TPU v7x, 128 devices: a whole 4x4x4 slice. The times are simulated.
128 devices in a mesh: row: 8 (over z, core), col: 16 (over y, x).
Axes of the slice: x: 4, y: 4, z: 4, core: 2. Of those that a mesh axis runs over, the one named last changes fastest.
Arguments:
- parent_cov: bfloat16 [32768, 32768], P(('row', 'col')), may hold values from -6 to 6
- anc_index: int32 [16384], replicated, may hold values from 0 to 32767, as said below
- fac_rows: bfloat16 [16384, 2048], P('col'), may hold values from -0.125 to 0.125
- inv_factor: bfloat16 [2048, 2048], P(None, 'row'), may hold values from -0.125 to 0.125
- own_inverse: float32 [2048, 2048], P('row', 'col'), may hold values from -6 to 6
Outputs:
- cov_sa: float32 [2048, 16384], P('row', 'col')
- cov_ss: float32 [2048, 2048], P('row', 'col')
Inputs may be any that keep to these rules, and one draw needn't show every extreme that they name: `anc_index`: all values are distinct. Split the list into aligned blocks of 2048 entries and the values into ranges of 256 (one device's rows of parent_cov): no block holds more than 32 values of one range, and every block holds exactly 32 values of some range.
All inputs are finite; a program needn't handle non-finite values.
Results may differ from a plain program's by a relative error of at most 0.0049.
Values may be sent and summed in bfloat16 or wider, within the bound.
No kernel may reach another device: no remote copies, remote signals or barrier semaphores. Data moves between devices by JAX's collectives and lax.ppermute only.
A program may use at most 192 MiB of HBM per device.

v0:
```python
import functools

import jax
import jax.numpy as jnp
from jax import lax
from jax.experimental import pallas as pl
from jax.experimental.pallas import tpu as pltpu
from jax.sharding import PartitionSpec as P

BF = jnp.bfloat16
F32 = jnp.float32
I32 = jnp.int32
SLOT = 32
LANES = 128
REACH = 10
LINES = 32
WIN = 256

def dot_nt(a, b):
    return lax.dot_general(a, b, (((1,), (1,)), ((), ())), preferred_element_type=F32)


def dot(a, b):
    return jnp.dot(a, b, preferred_element_type=F32)


def iota(shape, axis):
    return lax.broadcasted_iota(I32, shape, axis)


def ones_where(cond):
    return jnp.where(cond, 1.0, 0.0).astype(BF)


def index_kernel(tiles, anc_ref, slots_ref, table_ref, first_ref, count_ref):
    owners, rows = slots_ref.shape
    chunk = anc_ref.shape[1]
    tile_of = jnp.zeros((owners, rows), F32)
    for j in range(anc_ref.shape[0]):
        ids = anc_ref[j:j + 1, :]
        owner, inner = ids // rows, ids % rows
        tile = ((iota((1, chunk), 1) + j * chunk) // (anc_ref.shape[0] * chunk // tiles) + 1).astype(F32)
        owner_hot = jnp.where(iota((owners, chunk), 0) == owner, tile, 0.0).astype(BF)
        inner_hot = ones_where(iota((rows, chunk), 0) == inner)
        tile_of = tile_of + dot_nt(owner_hot, inner_hot)
    at = iota((rows, rows + LANES), 1)
    before = ones_where((iota((rows, rows + LANES), 0) < at) | (at >= rows))
    below = ones_where(iota((owners, owners), 1) < iota((owners, owners), 0))
    per_line = LANES // SLOT
    lines = owners // per_line
    pick = ones_where(iota((lines, owners), 1) // per_line == iota((lines, owners), 0))
    spread = iota((owners, LANES), 0) % per_line == iota((owners, LANES), 1) // SLOT
    s = (iota((lines, LANES), 1) % SLOT).astype(F32)
    edge = (iota((owners, LANES), 1) * WIN).astype(F32)
    expand = lambda v: dot(pick, jnp.where(spread, v, 0.0).astype(BF))
    slots = jnp.zeros((owners, rows), F32) - 1.0
    tile_len = float(anc_ref.shape[0] * chunk // tiles)
    prev = None
    for c in range(tiles):
        mask = tile_of == float(c + 1)
        both = dot(ones_where(mask), before)
        ahead, number = both[:, :rows], both[:, rows:]
        start = dot(below, number.astype(BF))
        base = float(c // 2 * SLOT + 1)
        lift = ahead + base
        if c % 2:
            lift = lift + jnp.concatenate([prev[0]] * (rows // LANES), axis=1)
        slots = slots + jnp.where(mask, lift, 0.0)
        high = jnp.floor(start * (1.0 / 32.0))
        n = expand(number)
        p = expand(high) * 32.0 + expand(start - high * 32.0)
        end = start + number
        lead = jnp.sum(jnp.where(end <= edge, 1.0, 0.0), axis=0, keepdims=True).astype(I32)
        last = jnp.sum(jnp.where(start < edge + float(WIN), 1.0, 0.0), axis=0, keepdims=True).astype(I32) - 1
        first = lead // per_line
        first_ref[c:c + 1, :] = first
        count_ref[c:c + 1, :] = (last // per_line - first) // REACH + 1
        if c % 2:
            n0, p0 = prev[1], prev[2]
            to = jnp.where(s < n0, p0 + s, jnp.where(s < n0 + n, tile_len + p + s - n0, -1.0))
            table_ref[c // 2, 0:lines, :] = to.astype(I32)
        prev = (number, n, p)
    slots_ref[...] = slots.astype(I32)


def index_tables(anc, owners, rows, tiles):
    lines = owners * SLOT // LANES
    return pl.pallas_call(
        functools.partial(index_kernel, tiles),
        out_shape=(
            jax.ShapeDtypeStruct((owners, rows), I32),
            jax.ShapeDtypeStruct((tiles // 2, lines, LANES), I32),
            jax.ShapeDtypeStruct((tiles, LANES), I32),
            jax.ShapeDtypeStruct((tiles, LANES), I32),
        ),
        cost_estimate=pl.CostEstimate(flops=8 << 30, bytes_accessed=1 << 20, transcendentals=0),
        name="index_tables",
    )(anc.reshape(-1, 2048))


def one_hot(targets, base):
    ids = iota((WIN, targets.shape[-1]), 0) + base
    return ones_where(ids == targets)


def window_hot(table, lead, first, base):
    start = jnp.minimum(first, LINES - REACH)
    lines = []
    for i in range(REACH):
        line = table[lead + (pl.ds(start + i, 1), slice(None))]
        lines.append(one_hot(jnp.where(start + i < first, -1, line), base))
    return start, jnp.concatenate(lines, axis=1)


def sort_kernel(per_step, slots_ref, cov_ref, out_ref):
    cols = slots_ref.shape[-1]
    for k in range(per_step):
        hot = one_hot(slots_ref[pl.ds(pl.program_id(0) * per_step + k, 1), :], 0)
        part = dot_nt(hot, cov_ref[:, k * cols:(k + 1) * cols]).astype(BF)
        for b in range(out_ref.shape[0]):
            out_ref[b, k * SLOT:(k + 1) * SLOT, :] = part[b * SLOT:(b + 1) * SLOT]


def sort_columns(cov, slots, blocks, per_step=16):
    rows, width = cov.shape
    ranges, cols = slots.shape
    return pl.pallas_call(
        functools.partial(sort_kernel, per_step),
        grid=(ranges // per_step,),
        in_specs=[
            pl.BlockSpec(slots.shape, lambda i: (0, 0)),
            pl.BlockSpec((rows, per_step * cols), lambda i: (0, i)),
        ],
        out_specs=pl.BlockSpec((blocks, per_step * SLOT, rows), lambda i: (0, i, 0)),
        out_shape=jax.ShapeDtypeStruct((blocks, ranges * SLOT, rows), BF),
        cost_estimate=pl.CostEstimate(flops=12 << 30, bytes_accessed=32 << 20, transcendentals=0),
        name="sort_columns",
    )(slots, cov)


def pack_kernel(first_ref, count_ref, dev_ref, slots_ref, table_ref, data_ref, out_ref, acc):
    block = pl.program_id(0)
    blocks, group, _, width = out_ref.shape
    windows = width // WIN
    rows_hot = one_hot(slots_ref[pl.ds(dev_ref[0], 1), :], 0)

    def part(first, base):
        start, hot = window_hot(table_ref, (block,), first, base)
        at = pl.multiple_of(start * LANES, LANES)
        return dot(hot, data_ref[0, pl.ds(at, REACH * LANES), :]).astype(BF)

    for job in range(group * windows):
        tile = block * group + job // windows
        acc[job * WIN:(job + 1) * WIN, :] = part(first_ref[tile, job % windows], job * WIN)

    def extra(job, carry):
        tile, w = block * group + job // windows, lax.rem(job, windows)
        at = pl.multiple_of(job * WIN, WIN)

        def more(i, carry):
            acc[pl.ds(at, WIN), :] += part(first_ref[tile, w] + i * REACH, at)
            return carry

        return lax.fori_loop(1, count_ref[tile, w], more, carry)

    lax.fori_loop(0, group * windows, extra, 0)
    for g in range(group):
        out = dot_nt(rows_hot, acc[g * width:(g + 1) * width, :]).astype(BF)
        for b in range(blocks):
            out_ref[b, g] = out[b * SLOT:(b + 1) * SLOT]


def pack_columns(data, slots, table, firsts, counts, device, tile_cols):
    blocks, length, rows = data.shape
    tiles = firsts.shape[0]
    group = tiles // blocks
    grid_spec = pltpu.PrefetchScalarGridSpec(
        num_scalar_prefetch=3,
        grid=(blocks,),
        in_specs=[
            pl.BlockSpec(slots.shape, lambda i, f, n, d: (0, 0)),
            pl.BlockSpec(table.shape, lambda i, f, n, d: (0, 0, 0)),
            pl.BlockSpec((1, length, rows), lambda i, f, n, d: (i, 0, 0)),
        ],
        out_specs=pl.BlockSpec((blocks, group, SLOT, tile_cols), lambda i, f, n, d: (0, i, 0, 0)),
        scratch_shapes=[pltpu.VMEM((group * tile_cols, rows), BF)],
    )
    return pl.pallas_call(
        pack_kernel,
        grid_spec=grid_spec,
        out_shape=jax.ShapeDtypeStruct((blocks, tiles, SLOT, tile_cols), BF),
        cost_estimate=pl.CostEstimate(flops=12 << 30, bytes_accessed=24 << 20, transcendentals=0),
        name="pack_columns",
    )(firsts, counts, device, slots, table, data)


def load_lhs(z, u_ref, lhs, sems):
    rows, cols = u_ref.shape[1:]
    return [
        pltpu.make_async_copy(
            u_ref.at[4 * z + 2 * half + core],
            lhs.at[pl.ds(core * rows, rows), pl.ds(half * cols, cols)],
            sems.at[2 * half + core],
        )
        for half in range(2) for core in range(2)
    ]


def start_loads(steps, pos_ref, u_ref, lhs, sems):
    jobs = []
    for n, step in enumerate(steps):
        jobs.append(load_lhs(lax.rem(pos_ref[0] + step, 4), u_ref, lhs.at[n], sems.at[n]))
        for copy in jobs[n]:
            copy.start()
    return jobs


def multiply(jobs, lhs, tile_ref, core, keep_ref, give_ref):
    half = keep_ref.shape[2]
    give = pl.multiple_of((1 - core) * half, half)
    keep = pl.multiple_of(core * half, half)
    for n, copies in enumerate(jobs):
        for copy in copies:
            copy.wait()
        give_ref[n] = dot(lhs[n], tile_ref[:, pl.ds(give, half)])
        keep_ref[n] = dot(lhs[n], tile_ref[:, pl.ds(keep, half)])


def first_kernel(steps, pos_ref, first_ref, count_ref, table_ref, got_ref, u_ref,
                 tile_ref, keep_ref, give_ref, held, lhs, got_sem, lhs_sems):
    z, core = pos_ref[0], pos_ref[1]
    load = pltpu.make_async_copy(got_ref, held, got_sem)
    load.start()
    jobs = start_loads(steps, pos_ref, u_ref, lhs, lhs_sems)
    per_line = LANES // SLOT
    span = REACH * per_line
    windows = tile_ref.shape[0] // WIN
    block = 2 * z + core

    def part(first, base):
        start, hot = window_hot(table_ref, (block,), first, base)
        data = held[pl.ds(start * per_line, span)].reshape(REACH * LANES, held.shape[-1])
        return dot(hot, data).astype(BF)

    load.wait()
    for w in range(windows):
        tile, v = 2 * block + w // (windows // 2), w % (windows // 2)
        tile_ref[w * WIN:(w + 1) * WIN, :] = part(first_ref[tile, v], w * WIN)

    def window(w, carry):
        tile, v = 2 * block + w // (windows // 2), lax.rem(w, windows // 2)
        at = pl.multiple_of(w * WIN, WIN)

        def more(i, carry):
            tile_ref[pl.ds(at, WIN), :] += part(first_ref[tile, v] + i * REACH, at)
            return carry

        return lax.fori_loop(1, count_ref[tile, v], more, carry)

    lax.fori_loop(0, windows, window, 0)
    multiply(jobs, lhs, tile_ref, core, keep_ref, give_ref)


def next_kernel(steps, pos_ref, u_ref, tile_ref, keep_ref, give_ref, lhs, sems):
    jobs = start_loads(steps, pos_ref, u_ref, lhs, sems)
    multiply(jobs, lhs, tile_ref, pos_ref[1], keep_ref, give_ref)


def first_shares(steps, position, firsts, counts, table, received, u_block):
    owners, _, cols = received.shape
    rows, depth = 2 * u_block.shape[1], 2 * u_block.shape[2]
    smem = pl.BlockSpec(memory_space=pltpu.SMEM)
    vmem = pl.BlockSpec(memory_space=pltpu.VMEM)
    hbm = pl.BlockSpec(memory_space=pl.ANY)
    share = jax.ShapeDtypeStruct((len(steps), rows, cols // 2), F32)
    return pl.pallas_call(
        functools.partial(first_kernel, steps),
        in_specs=[smem, smem, smem, vmem, hbm, hbm],
        out_specs=(vmem, vmem, vmem),
        out_shape=(jax.ShapeDtypeStruct((depth, cols), BF), share, share),
        scratch_shapes=[
            pltpu.VMEM((owners, SLOT, cols), BF),
            pltpu.VMEM((len(steps), rows, depth), BF),
            pltpu.SemaphoreType.DMA,
            pltpu.SemaphoreType.DMA((len(steps), 4)),
        ],
        cost_estimate=pl.CostEstimate(flops=24 << 30, bytes_accessed=24 << 20, transcendentals=0),
        name="squeeze_and_first_shares",
    )(position, firsts, counts, table, received, u_block)


def next_shares(steps, position, u_block, tile):
    depth, cols = tile.shape
    rows = 2 * u_block.shape[1]
    smem = pl.BlockSpec(memory_space=pltpu.SMEM)
    vmem = pl.BlockSpec(memory_space=pltpu.VMEM)
    hbm = pl.BlockSpec(memory_space=pl.ANY)
    share = jax.ShapeDtypeStruct((len(steps), rows, cols // 2), F32)
    return pl.pallas_call(
        functools.partial(next_kernel, steps),
        in_specs=[smem, hbm, vmem],
        out_specs=(vmem, vmem),
        out_shape=(share, share),
        scratch_shapes=[
            pltpu.VMEM((len(steps), rows, depth), BF),
            pltpu.SemaphoreType.DMA((len(steps), 4)),
        ],
        cost_estimate=pl.CostEstimate(flops=12 << 30, bytes_accessed=16 << 20, transcendentals=0),
        name="next_shares",
    )(position, u_block, tile)


def pairs(target):
    result = []
    for r in range(8):
        for c in range(16):
            z, core, y, x = target(r // 2, r % 2, c // 4, c % 4)
            result.append((r * 16 + c, (2 * z + core) * 16 + 4 * y + x))
    return result


def local(parent_cov, anc_index, fac_rows, inv_factor, own_inverse):
    row_count = lax.axis_size("row")
    col_count = lax.axis_size("col")
    owners = row_count * col_count
    parent_rows = parent_cov.shape[0]
    tile_cols = anc_index.shape[0] // col_count
    sep_cols = inv_factor.shape[1]
    row_index = lax.axis_index("row")
    col_index = lax.axis_index("col")
    core = row_index % 2
    device = jnp.reshape(row_index * col_count + col_index, (1,)).astype(I32)
    position = jnp.stack([row_index // 2, core]).astype(I32)
    both = ("row", "col")
    swap = pairs(lambda z, core, y, x: (z, 1 - core, y, x))

    own_ids = lax.dynamic_slice_in_dim(anc_index, col_index * tile_cols, tile_cols)
    rank = jnp.sum((own_ids[None, :] < own_ids[:, None]).astype(I32), axis=1)
    perm = (jnp.arange(tile_cols, dtype=I32)[:, None] == rank[None, :]).astype(BF)
    row_ids = jnp.arange(inv_factor.shape[0], dtype=I32)[:, None]
    col_ids = row_index * sep_cols + jnp.arange(sep_cols, dtype=I32)[None, :]
    lower = jnp.where(row_ids >= col_ids, inv_factor, jnp.zeros((), inv_factor.dtype))
    u_tile = jnp.dot(fac_rows, lower, preferred_element_type=F32).astype(BF)
    u_t = lax.dot_general(
        u_tile, perm, (((0,), (1,)), ((), ())), preferred_element_type=F32
    ).astype(BF)
    piece = lax.ppermute(
        u_t, both, pairs(lambda z, core, y, x: (y, x // 2, z, 2 * (x % 2) + core))
    )
    slots, table, firsts, counts = index_tables(anc_index, owners, parent_rows, col_count)
    data = sort_columns(parent_cov, slots, row_count)
    piece, data = lax.optimization_barrier((piece, data))
    u_block = lax.all_gather(piece, "col", axis=0)
    outgoing = pack_columns(data, slots, table, firsts, counts, device, tile_cols)
    outgoing, u_t = lax.optimization_barrier((outgoing, u_t))
    u_cols = lax.all_gather(u_t, "row", axis=0, tiled=True)
    flat_out = outgoing.reshape(owners * SLOT, tile_cols)
    received = lax.all_to_all(flat_out, both, split_axis=0, concat_axis=0, tiled=True)
    received = received.reshape(owners, SLOT, tile_cols)

    tile, keep, give = first_shares((2, 1), position, firsts, counts, table, received, u_block)
    first = (keep + lax.ppermute(give, both, swap)).astype(BF)
    keep, give = next_shares((3, 0), position, u_block, tile)
    second = keep + lax.ppermute(give, both, swap)
    total = second[1]
    for step, share in ((2, first[0]), (1, first[1]), (3, second[0].astype(BF))):
        share = lax.ppermute(
            share, both, pairs(lambda z, core, y, x, step=step: ((z + step) % 4, core, y, x))
        )
        total = total + share.astype(F32)
    total = -total
    kept = lax.dynamic_slice_in_dim(total, core * sep_cols, sep_cols, axis=0)
    given = lax.dynamic_slice_in_dim(total, (1 - core) * sep_cols, sep_cols, axis=0)
    taken = lax.ppermute(given, both, swap)
    sa_sorted = jnp.concatenate(
        [jnp.where(core == 0, kept, taken), jnp.where(core == 0, taken, kept)], axis=1
    )

    sa_high = sa_sorted.astype(BF)
    ss_part = dot_nt(u_cols, sa_high).astype(BF)
    ss_all = lax.all_to_all(ss_part, "col", split_axis=0, concat_axis=0, tiled=True)
    sa_low = (sa_sorted - sa_high.astype(F32)).astype(BF)
    cov_sa = dot(sa_high, perm) + dot(sa_low, perm)
    ss_sum = jnp.sum(ss_all.reshape(col_count, -1, ss_all.shape[1]).astype(F32), axis=0)
    cov_ss = own_inverse - ss_sum.T
    return (cov_sa, cov_ss)


def solution(mesh):
    return jax.shard_map(
        local,
        mesh=mesh,
        in_specs=(P(("row", "col"), None), P(), P("col", None), P(None, "row"), P("row", "col")),
        out_specs=(P("row", "col"), P("row", "col")),
        check_vma=False,
    )
```

profile of v0, /device:TPU:0, one launch (start us, length us, event | category | flops | bytes accessed | tf_op | source)
XLA Modules:
  0.0 308.5 jit_solution(10964262986136948645)
XLA Ops:
  7.2 0.7 dynamic_slice.9
  7.9 0.6 convert_reduce_fusion
  8.5 4.6 %fusion.8 = bf16[256,1024]{1,0:T(8,128)(2,1)S(1)} fusion(s32[1024]{0:T(1024)S(1)} %convert_reduce_fusion, bf16[1024,2048]{1,0:T(8,128)(2,1)} %param.7, bf16[2048,256]{1,0:T(8,128)(2,1)} %param.8, s32[256]{0:T(256)S(1)} %iota_add_fusion), kind=kOutput, calls=%fused_computation.14 | convolution fusion | flops 1613234176 | bytes 5772288 | tf_op jit(solution)/shard_map/dot_general | solution.py:344
  13.1 0.7 collective-permute-start
  13.8 0.6 reshape.29.anc_ref
  14.5 11.2 %index_tables.1 = (s32[128,256]{1,0:T(8,128)}, s32[8,32,128]{2,1,0:T(8,128)}, s32[16,128]{1,0:T(8,128)}, s32[16,128]{1,0:T(8,128)}) custom-call(s32[8,2048]{1,0:T(8,128)} %reshape.29.anc_ref), custom_call_target="tpu_custom_call" | custom-call | flops 8589934592 | bytes 1048576 | tf_op jit(solution)/shard_map/index_tables/pallas_call | solution.py:88
  25.7 16.0 %sort_columns.1.data_ref = bf16[8,4096,256]{2,1,0:T(8,128)(2,1)} custom-call(s32[128,256]{1,0:T(8,128)} %get-tuple-element.15.slots_ref, bf16[256,32768]{1,0:T(8,128)(2,1)} %cov_ref.1), custom_call_target="tpu_custom_call" | custom-call | flops 12884901888 | bytes 33554432 | tf_op jit(solution)/shard_map/sort_columns/pallas_call | solution.py:127
  41.7 0.8 copy-done.4
  42.5 21.6 %pack_columns.1 = bf16[8,16,32,1024]{3,2,1,0:T(8,128)(2,1)} custom-call(s32[16,128]{1,0:T(8,128)} %get-tuple-element.17.first_ref, s32[16,128]{1,0:T(8,128)} %get-tuple-element.18.count_ref, s32[1]{0:T(128)} %bitcast.3.dev_ref, s32[128,256]{1,0:T(8,128)} %get-tuple-element.15.slots_ref, s32[8,32,128]{2,1,0:T(8,128)} %get-tuple-element.19.table_ref, ...), custom_call_target="tpu_custom_call" | custom-call | flops 12884901888 | bytes 25165824 | tf_op jit(solution)/shard_map/pack_columns/pallas_call | solution.py:188
  64.1 14.1 %all-to-all-start = ((bf16[128,32,1024]{2,1,0:T(8,128)(2,1)}), bf16[128,32,1024]{2,1,0:T(8,128)(2,1)}, u32[]{:S(2)}, u32[]{:S(2)}) async-start(bf16[128,32,1024]{2,1,0:T(8,128)(2,1)} %bitcast.26), calls=%async_computation | async-start | bytes 16777216 | tf_op jit(solution)/shard_map/all_to_all | solution.py:358
  78.2 0.2 all-gather.4.cloned.1.call-start
  78.5 0.6 pad_add_fusion.pos_ref
  79.1 128.8 %all-to-all-done.got_ref = bf16[128,32,1024]{2,1,0:T(8,128)(2,1)} async-done(((bf16[128,32,1024]{2,1,0:T(8,128)(2,1)}), bf16[128,32,1024]{2,1,0:T(8,128)(2,1)}, u32[]{:S(2)}, u32[]{:S(2)}) %all-to-all-start) | async-done | bytes 8388640 | tf_op jit(solution)/shard_map/all_to_all | solution.py:358
  207.9 18.9 %squeeze_and_first_shares.1 = (bf16[2048,1024]{1,0:T(8,128)(2,1)}, f32[2,512,512]{2,1,0:T(8,128)}, f32[2,512,512]{2,1,0:T(8,128)}) custom-call(s32[2]{0:T(128)} %pad_add_fusion.pos_ref, s32[16,128]{1,0:T(8,128)} %get-tuple-element.17.first_ref, s32[16,128]{1,0:T(8,128)} %get-tuple-element.18.count_ref, s32[8,32,128]{2,1,0:T(8,128)} %get-tuple-element.19.table_ref, ...), custom_call_target="tpu_custom_call" | custom-call | flops 25769803776 | bytes 25165824 | tf_op jit(solution)/shard_map/squeeze_and_first_shares/pallas_call | solution.py:276
  226.9 10.1 %next_shares.1 = (f32[2,512,512]{2,1,0:T(8,128)}, f32[2,512,512]{2,1,0:T(8,128)}) custom-call(s32[2]{0:T(128)} %pad_add_fusion.pos_ref, bf16[16,256,1024]{2,1,0:T(8,128)(2,1)} %bitcast.28, bf16[2048,1024]{1,0:T(8,128)(2,1)} %get-tuple-element.22.tile_ref), custom_call_target="tpu_custom_call" | custom-call | flops 12884901888 | bytes 16777216 | tf_op jit(solution)/shard_map/next_shares/pallas_call | solution.py:299
  237.0 0.5 collective-permute-start.1
  237.5 2.0 add_convert_fusion
  239.6 1.0 slice_bitcast_fusion.2
  240.6 0.7 collective-permute-start.3
  241.3 1.0 collective-permute-start.4
  242.3 0.5 add.51
  242.9 2.3 collective-permute-start.5
  245.2 12.0 %collective-permute-done.3 = bf16[512,512]{1,0:T(8,128)(2,1)S(1)} collective-permute-done((bf16[512,512]{1,0:T(8,128)(2,1)}, bf16[512,512]{1,0:T(8,128)(2,1)S(1)}, u32[]{:S(2)}, u32[]{:S(2)}) %collective-permute-start.3) | collective-permute-done | bytes 524320 | tf_op jit(solution)/shard_map/ppermute | solution.py:367
  257.2 10.4 %collective-permute-done.4 = bf16[512,512]{1,0:T(8,128)(2,1)} collective-permute-done((bf16[512,512]{1,0:T(8,128)(2,1)}, bf16[512,512]{1,0:T(8,128)(2,1)}, u32[]{:S(2)}, u32[]{:S(2)}) %collective-permute-start.4) | collective-permute-done | bytes 524320 | tf_op jit(solution)/shard_map/ppermute | solution.py:367
  267.6 1.6 fusion.13
  269.4 1.9 collective-permute-done.6
  271.5 4.7 %convolution_convert_fusion = bf16[2048,256]{1,0:T(8,128)(2,1)} fusion(bf16[2048,1024]{1,0:T(8,128)(2,1)} %all-gather.4.cloned.1.call-done, f32[256,512]{1,0:T(8,128)S(1)} %get-tuple-element.33, f32[256,512]{1,0:T(8,128)S(1)} %get-tuple-element.32), kind=kOutput, calls=%fused_computation.5 | convolution fusion | flops 1075314688 | bytes 6291456 | tf_op jit(solution)/shard_map/dot_general | solution.py:20
  276.2 6.7 %all-to-all-start.1 = ((bf16[16,128,256]{2,1,0:T(8,128)(2,1)}), bf16[16,128,256]{2,1,0:T(8,128)(2,1)S(1)}, u32[]{:S(2)}, u32[]{:S(2)}) async-start(bf16[16,128,256]{2,1,0:T(8,128)(2,1)} %bitcast.9), calls=%async_computation.1 | async-start | bytes 2097152 | tf_op jit(solution)/shard_map/all_to_all | solution.py:381
  283.0 2.2 fusion
  285.2 2.0 fusion.7
  287.2 13.5 %all-to-all-done.1 = bf16[16,128,256]{2,1,0:T(8,128)(2,1)S(1)} async-done(((bf16[16,128,256]{2,1,0:T(8,128)(2,1)}), bf16[16,128,256]{2,1,0:T(8,128)(2,1)S(1)}, u32[]{:S(2)}, u32[]{:S(2)}) %all-to-all-start.1) | async-done | bytes 1048608 | tf_op jit(solution)/shard_map/all_to_all | solution.py:381
  300.9 0.8 copy.10
  (35 shorter events, 0.8 us)
Async XLA Ops:
  7.2 200.7 %all-gather.6.cloned.1.call-start = ((), (), s32[]{:S(2)}) async-start(), calls=%async_computation.3 | async-start | bytes 8912896 | tf_op jit(solution)/shard_map/all_gather | solution.py:353
  8.5 5.4 %copy-start.8 = (s32[16384]{0:T(1024)S(1)}, s32[16384]{0:T(1024)}, u32[]{:S(2)}) copy-start(s32[16384]{0:T(1024)} %param.6) | copy-start | bytes 196612
  13.1 12.6 %copy-start.3 = (bf16[256,1024]{1,0:T(8,128)(2,1)}, bf16[256,1024]{1,0:T(8,128)(2,1)S(1)}, u32[]{:S(2)}) copy-start(bf16[256,1024]{1,0:T(8,128)(2,1)S(1)} %fusion.8) | copy-start | bytes 1572868
  13.1 28.6 %collective-permute-start = (bf16[256,1024]{1,0:T(8,128)(2,1)S(1)}, bf16[256,1024]{1,0:T(8,128)(2,1)S(1)}, u32[]{:S(2)}, u32[]{:S(2)}) collective-permute-start(bf16[256,1024]{1,0:T(8,128)(2,1)S(1)} %fusion.8), channel_id=1, source_target_pairs={{0,0},{1,2},{2,16},{3,18},{4,32},{5,34},{6,48},{7,50},{8,64},{9,66... | collective-permute-start | bytes 1572872 | tf_op jit(solution)/shard_map/ppermute | solution.py:347
  41.7 0.8 copy-start.4
  64.1 143.8 %all-to-all-start = ((bf16[128,32,1024]{2,1,0:T(8,128)(2,1)}), bf16[128,32,1024]{2,1,0:T(8,128)(2,1)}, u32[]{:S(2)}, u32[]{:S(2)}) async-start(bf16[128,32,1024]{2,1,0:T(8,128)(2,1)} %bitcast.26), calls=%async_computation | async-start | bytes 16777216 | tf_op jit(solution)/shard_map/all_to_all | solution.py:358
  78.2 193.3 %all-gather.4.cloned.1.call-start = ((), (), s32[]{:S(2)}) async-start(), calls=%async_computation.2 | async-start | bytes 4718592 | tf_op jit(solution)/shard_map/all_gather | solution.py:356
  226.8 10.8 %collective-permute-start.2 = (f32[2,512,512]{2,1,0:T(8,128)}, f32[2,512,512]{2,1,0:T(8,128)}, u32[]{:S(2)}, u32[]{:S(2)}) collective-permute-start(f32[2,512,512]{2,1,0:T(8,128)} %get-tuple-element.26), channel_id=1, source_target_pairs={{0,16},{1,17},{2,18},{3,19},{4,20},{5,21},{6,22},{7,23},{8,24},{9,... | collective-permute-start | bytes 6291464 | tf_op jit(solution)/shard_map/ppermute | solution.py:362
  226.9 10.7 %copy-start.1 = (f32[2,512,512]{2,1,0:T(8,128)S(1)}, f32[2,512,512]{2,1,0:T(8,128)}, u32[]{:S(2)}) copy-start(f32[2,512,512]{2,1,0:T(8,128)} %get-tuple-element.25) | copy-start | bytes 6291460
  237.0 5.3 %copy-start = (f32[2,512,512]{2,1,0:T(8,128)S(1)}, f32[2,512,512]{2,1,0:T(8,128)}, u32[]{:S(2)}) copy-start(f32[2,512,512]{2,1,0:T(8,128)} %get-tuple-element.23) | copy-start | bytes 6291460
  237.0 5.3 %collective-permute-start.1 = (f32[2,512,512]{2,1,0:T(8,128)}, f32[2,512,512]{2,1,0:T(8,128)S(1)}, u32[]{:S(2)}, u32[]{:S(2)}) collective-permute-start(f32[2,512,512]{2,1,0:T(8,128)} %get-tuple-element.24), channel_id=1, source_target_pairs={{0,16},{1,17},{2,18},{3,19},{4,20},{5,21},{6,22},{7,23},{8,24},{9,... | collective-permute-start | bytes 6291464 | tf_op jit(solution)/shard_map/ppermute | solution.py:364
  240.6 16.5 %collective-permute-start.3 = (bf16[512,512]{1,0:T(8,128)(2,1)}, bf16[512,512]{1,0:T(8,128)(2,1)S(1)}, u32[]{:S(2)}, u32[]{:S(2)}) collective-permute-start(bf16[512,512]{1,0:T(8,128)(2,1)} %get-tuple-element.34), channel_id=1, source_target_pairs={{0,64},{1,65},{2,66},{3,67},{4,68},{5,69},{6,70},{7,71},{8,72},{9,... | collective-permute-start | bytes 1572872 | tf_op jit(solution)/shard_map/ppermute | solution.py:367
  241.3 26.3 %collective-permute-start.4 = (bf16[512,512]{1,0:T(8,128)(2,1)}, bf16[512,512]{1,0:T(8,128)(2,1)}, u32[]{:S(2)}, u32[]{:S(2)}) collective-permute-start(bf16[512,512]{1,0:T(8,128)(2,1)} %get-tuple-element.35), channel_id=1, source_target_pairs={{0,32},{1,33},{2,34},{3,35},{4,36},{5,37},{6,38},{7,39},{8,40},{9,... | collective-permute-start | bytes 1572872 | tf_op jit(solution)/shard_map/ppermute | solution.py:367
  242.9 24.8 %collective-permute-start.5 = (bf16[512,512]{1,0:T(8,128)(2,1)S(1)}, bf16[512,512]{1,0:T(8,128)(2,1)}, u32[]{:S(2)}, u32[]{:S(2)}) collective-permute-start(bf16[512,512]{1,0:T(8,128)(2,1)S(1)} %fusion.18), channel_id=1, source_target_pairs={{0,96},{1,97},{2,98},{3,99},{4,100},{5,101},{6,102},{7,103},{8,104... | collective-permute-start | bytes 1572872 | tf_op jit(solution)/shard_map/ppermute | solution.py:367
  257.2 10.4 %copy-start.2 = (bf16[512,512]{1,0:T(8,128)(2,1)}, bf16[512,512]{1,0:T(8,128)(2,1)S(1)}, u32[]{:S(2)}) copy-start(bf16[512,512]{1,0:T(8,128)(2,1)S(1)} %collective-permute-done.3) | copy-start | bytes 1572868
  269.3 2.0 collective-permute-start.6
  271.5 4.7 %copy-start.5 = (f32[256,512]{1,0:T(8,128)}, f32[256,512]{1,0:T(8,128)S(1)}, u32[]{:S(2)}) copy-start(f32[256,512]{1,0:T(8,128)S(1)} %get-tuple-element.33) | copy-start | bytes 1572868
  271.5 11.4 %copy-start.7 = (f32[256,128]{1,0:T(8,128)S(1)}, f32[256,128]{1,0:T(8,128)}, u32[]{:S(2)}) copy-start(f32[256,128]{1,0:T(8,128)} %param.9) | copy-start | bytes 393220
  276.2 24.5 %all-to-all-start.1 = ((bf16[16,128,256]{2,1,0:T(8,128)(2,1)}), bf16[16,128,256]{2,1,0:T(8,128)(2,1)S(1)}, u32[]{:S(2)}, u32[]{:S(2)}) async-start(bf16[16,128,256]{2,1,0:T(8,128)(2,1)} %bitcast.9), calls=%async_computation.1 | async-start | bytes 2097152 | tf_op jit(solution)/shard_map/all_to_all | solution.py:381
  282.9 2.3 copy-start.6
Sparse Core Ops, SparseCore 0:
  42.6 156.0 all-gather.5
  200.4 36.9 all-gather.3
where the time goes:
time: 309 us; the launch traced here: 308 us
  waiting for transfers between devices  167 us (54%)
  Pallas kernels  77.8 us (25%)
  starting transfers between devices  26.4 us (9%)
  between operations  14.3 us (5%)
  matrix products  13.5 us (4%)
  other arithmetic  5.58 us (2%)
  local copies, waits for them, and re-layouts  4.18 us (1%)
    all_to_all x1, waiting for transfers between devices, local(): lax.all_to_all(flat_out, both, split_axis=0, concat_axis=0, tiled=True)  129 us
    ppermute x3, waiting for transfers between devices, local(): lax.ppermute(share, both, pairs(lambda z, core, y, x, step=step: ((z + st...  22.4 us
    pallas_call x1, Pallas kernels, pack_columns(): pl.pallas_call(pack_kernel, grid_spec=grid_spec, out_shape=jax.ShapeDtype...  21.6 us
    pallas_call x1, Pallas kernels, first_shares(): pl.pallas_call(functools.partial(first_kernel, steps), in_specs=[smem, sm...  18.9 us
    pallas_call x1, Pallas kernels, sort_columns(): pl.pallas_call(functools.partial(sort_kernel, per_step), grid=(ranges //...  16 us
    all_to_all x1, starting transfers between devices, local(): lax.all_to_all(flat_out, both, split_axis=0, concat_axis=0, tiled=True)  14.1 us
    all_to_all x1, waiting for transfers between devices, local(): lax.all_to_all(ss_part, 'col', split_axis=0, concat_axis=0, tiled=True)  13.5 us
    pallas_call x1, Pallas kernels, index_tables(): pl.pallas_call(functools.partial(index_kernel, tiles), out_shape=(jax.Sha...  11.2 us
  transfers between devices with their start and end apart: 11, of which 5 were waited for; matrix products, arithmetic and copies ran while one was open for 4% of the time, Pallas kernels for 25%

commit v1 on v0

--- a/solution.py
+++ b/solution.py
@@ -94,6 +94,7 @@
             jax.ShapeDtypeStruct((tiles, LANES), I32),
         ),
         cost_estimate=pl.CostEstimate(flops=8 << 30, bytes_accessed=1 << 20, transcendentals=0),
+        compiler_params=pltpu.CompilerParams(vmem_limit_bytes=24 << 20),
         name="index_tables",
     )(anc.reshape(-1, 2048))
 
@@ -117,11 +118,12 @@
     for k in range(per_step):
         hot = one_hot(slots_ref[pl.ds(pl.program_id(0) * per_step + k, 1), :], 0)
         part = dot_nt(hot, cov_ref[:, k * cols:(k + 1) * cols]).astype(BF)
+        at = pl.multiple_of((pl.program_id(0) * per_step + k) * SLOT, SLOT)
         for b in range(out_ref.shape[0]):
-            out_ref[b, k * SLOT:(k + 1) * SLOT, :] = part[b * SLOT:(b + 1) * SLOT]
-
-
-def sort_columns(cov, slots, blocks, per_step=16):
+            out_ref[b, pl.ds(at, SLOT), :] = part[b * SLOT:(b + 1) * SLOT]
+
+
+def sort_columns(cov, slots, blocks, per_step=32):
     rows, width = cov.shape
     ranges, cols = slots.shape
     return pl.pallas_call(
@@ -131,9 +133,10 @@
             pl.BlockSpec(slots.shape, lambda i: (0, 0)),
             pl.BlockSpec((rows, per_step * cols), lambda i: (0, i)),
         ],
-        out_specs=pl.BlockSpec((blocks, per_step * SLOT, rows), lambda i: (0, i, 0)),
-        out_shape=jax.ShapeDtypeStruct((blocks, ranges * SLOT, rows), BF),
+        out_specs=pl.BlockSpec(memory_space=pltpu.VMEM),
+        out_shape=pltpu.VMEM((blocks, ranges * SLOT, rows), BF),
         cost_estimate=pl.CostEstimate(flops=12 << 30, bytes_accessed=32 << 20, transcendentals=0),
+        compiler_params=pltpu.CompilerParams(vmem_limit_bytes=24 << 20),
         name="sort_columns",
     )(slots, cov)
 
@@ -147,7 +150,7 @@
     def part(first, base):
         start, hot = window_hot(table_ref, (block,), first, base)
         at = pl.multiple_of(start * LANES, LANES)
-        return dot(hot, data_ref[0, pl.ds(at, REACH * LANES), :]).astype(BF)
+        return dot(hot, data_ref[block, pl.ds(at, REACH * LANES), :]).astype(BF)
 
     for job in range(group * windows):
         tile = block * group + job // windows
@@ -163,7 +166,14 @@
 
         return lax.fori_loop(1, count_ref[tile, w], more, carry)
 
-    lax.fori_loop(0, group * windows, extra, 0)
+    most = count_ref[block * group, 0]
+    for job in range(1, group * windows):
+        most = jnp.maximum(most, count_ref[block * group + job // windows, job % windows])
+
+    @pl.when(most > 1)
+    def _():
+        lax.fori_loop(0, group * windows, extra, 0)
+
     for g in range(group):
         out = dot_nt(rows_hot, acc[g * width:(g + 1) * width, :]).astype(BF)
         for b in range(blocks):
@@ -180,7 +190,7 @@
         in_specs=[
             pl.BlockSpec(slots.shape, lambda i, f, n, d: (0, 0)),
             pl.BlockSpec(table.shape, lambda i, f, n, d: (0, 0, 0)),
-            pl.BlockSpec((1, length, rows), lambda i, f, n, d: (i, 0, 0)),
+            pl.BlockSpec(memory_space=pltpu.VMEM),
         ],
         out_specs=pl.BlockSpec((blocks, group, SLOT, tile_cols), lambda i, f, n, d: (0, i, 0, 0)),
         scratch_shapes=[pltpu.VMEM((group * tile_cols, rows), BF)],
@@ -190,6 +200,7 @@
         grid_spec=grid_spec,
         out_shape=jax.ShapeDtypeStruct((blocks, tiles, SLOT, tile_cols), BF),
         cost_estimate=pl.CostEstimate(flops=12 << 30, bytes_accessed=24 << 20, transcendentals=0),
+        compiler_params=pltpu.CompilerParams(vmem_limit_bytes=24 << 20),
         name="pack_columns",
     )(firsts, counts, device, slots, table, data)
 
@@ -277,7 +288,7 @@
         functools.partial(first_kernel, steps),
         in_specs=[smem, smem, smem, vmem, hbm, hbm],
         out_specs=(vmem, vmem, vmem),
-        out_shape=(jax.ShapeDtypeStruct((depth, cols), BF), share, share),
+        out_shape=(pltpu.VMEM((depth, cols), BF), share, share),
         scratch_shapes=[
             pltpu.VMEM((owners, SLOT, cols), BF),
             pltpu.VMEM((len(steps), rows, depth), BF),
@@ -285,6 +296,7 @@
             pltpu.SemaphoreType.DMA((len(steps), 4)),
         ],
         cost_estimate=pl.CostEstimate(flops=24 << 30, bytes_accessed=24 << 20, transcendentals=0),
+        compiler_params=pltpu.CompilerParams(vmem_limit_bytes=36 << 20),
         name="squeeze_and_first_shares",
     )(position, firsts, counts, table, received, u_block)
 
@@ -306,6 +318,7 @@
             pltpu.SemaphoreType.DMA((len(steps), 4)),
         ],
         cost_estimate=pl.CostEstimate(flops=12 << 30, bytes_accessed=16 << 20, transcendentals=0),
+        compiler_params=pltpu.CompilerParams(vmem_limit_bytes=24 << 20),
         name="next_shares",
     )(position, u_block, tile)
 

time: 309 us -> 310 us (level)
  Pallas kernels: 77.8 us -> 58.2 us
  local copies, waits for them, and re-layouts: 4.18 us -> 18.2 us
  starting transfers between devices: 26.4 us -> 37.5 us
    unnamed x20 -> x24, local copies, waits for them, and re-layouts: 1.69 us -> 16.4 us
    pallas_call x1, Pallas kernels: 16 us -> 8.73 us  [sort_columns(): pl.pallas_call(functools.partial(sort_kernel, per_step), grid=(ranges //...]
    all_to_all x1, starting transfers between devices: 6.71 us -> 11.5 us  [local(): lax.all_to_all(ss_part, 'col', split_axis=0, concat_axis=0, tiled=True)]
    pallas_call x1, Pallas kernels: 10.1 us -> 5.68 us  [next_shares(): pl.pallas_call(functools.partial(next_kernel, steps), in_specs=[smem, hbm...]
    ppermute x3, starting transfers between devices: 3.98 us -> 8.12 us  [local(): lax.ppermute(share, both, pairs(lambda z, core, y, x, step=step: ((z + st...]
    pallas_call x1, Pallas kernels: 21.6 us -> 17.9 us  [pack_columns(): pl.pallas_call(pack_kernel, grid_spec=grid_spec, out_shape=jax.ShapeDtype...]
  transfers between devices with their start and end apart: 11 -> 11, of which waited for: 5 -> 6; matrix products, arithmetic and copies ran while one was open for 4% -> 3% of each run, Pallas kernels for 25% -> 19%
where the time goes in v1:
time: 310 us
  waiting for transfers between devices  164 us (53%)
  Pallas kernels  58.2 us (19%)
  starting transfers between devices  37.5 us (12%)
  local copies, waits for them, and re-layouts  18.2 us (6%)
  between operations  14.4 us (5%)
  matrix products  13.5 us (4%)
  other arithmetic  3.6 us (1%)
    all_to_all x1, waiting for transfers between devices, local(): lax.all_to_all(flat_out, both, split_axis=0, concat_axis=0, tiled=True)  128 us
    ppermute x3, waiting for transfers between devices, local(): lax.ppermute(share, both, pairs(lambda z, core, y, x, step=step: ((z + st...  19.9 us
    pallas_call x1, Pallas kernels, pack_columns(): pl.pallas_call(pack_kernel, grid_spec=grid_spec, out_shape=jax.ShapeDtype...  17.9 us
    unnamed x24, local copies, waits for them, and re-layouts  16.4 us
    pallas_call x1, Pallas kernels, first_shares(): pl.pallas_call(functools.partial(first_kernel, steps), in_specs=[smem, sm...  16.2 us
    all_to_all x1, starting transfers between devices, local(): lax.all_to_all(flat_out, both, split_axis=0, concat_axis=0, tiled=True)  16 us
    all_to_all x1, waiting for transfers between devices, local(): lax.all_to_all(ss_part, 'col', split_axis=0, concat_axis=0, tiled=True)  13.5 us
    all_to_all x1, starting transfers between devices, local(): lax.all_to_all(ss_part, 'col', split_axis=0, concat_axis=0, tiled=True)  11.5 us
  transfers between devices with their start and end apart: 11, of which 6 were waited for; matrix products, arithmetic and copies ran while one was open for 3% of the time, Pallas kernels for 19%

profile of v1, /device:TPU:0, one launch (start us, length us, event | category | flops | bytes accessed | tf_op | source)
XLA Modules:
  0.0 309.5 jit_solution(3015705790875226813)
XLA Ops:
  7.2 0.7 dynamic_slice.9
  7.9 0.6 convert_reduce_fusion
  8.5 4.6 %fusion.8 = bf16[256,1024]{1,0:T(8,128)(2,1)S(1)} fusion(s32[1024]{0:T(1024)S(1)} %convert_reduce_fusion, bf16[1024,2048]{1,0:T(8,128)(2,1)} %param.7, bf16[2048,256]{1,0:T(8,128)(2,1)} %param.8, s32[256]{0:T(256)S(1)} %iota_add_fusion), kind=kOutput, calls=%fused_computation.14 | convolution fusion | flops 1613234176 | bytes 5772288 | tf_op jit(solution)/shard_map/dot_general | solution.py:357
  13.1 0.7 collective-permute-start
  13.9 9.7 %index_tables.1 = (s32[128,256]{1,0:T(8,128)S(1)}, s32[8,32,128]{2,1,0:T(8,128)S(1)}, s32[16,128]{1,0:T(8,128)S(1)}, s32[16,128]{1,0:T(8,128)S(1)}) custom-call(s32[8,2048]{1,0:T(8,128)S(1)} %reshape.29.anc_ref), custom_call_target="tpu_custom_call" | custom-call | flops 8589934592 | bytes 1048576 | tf_op jit(solution)/shard_map/index_tables/pallas_call | solution.py:88
  23.6 8.7 %sort_columns.1.data_ref = bf16[8,4096,256]{2,1,0:T(8,128)(2,1)S(1)} custom-call(s32[128,256]{1,0:T(8,128)S(1)} %get-tuple-element.15.slots_ref, bf16[256,32768]{1,0:T(8,128)(2,1)} %cov_ref.1), custom_call_target="tpu_custom_call" | custom-call | flops 12884901888 | bytes 33554432 | tf_op jit(solution)/shard_map/sort_columns/pallas_call | solution.py:129
  32.3 5.7 %copy-done.2 = bf16[8,4096,256]{2,1,0:T(8,128)(2,1)} copy-done((bf16[8,4096,256]{2,1,0:T(8,128)(2,1)}, bf16[8,4096,256]{2,1,0:T(8,128)(2,1)S(1)}, u32[]{:S(2)}) %copy-start.2) | copy-done | bytes 16777240
  38.0 0.8 copy-done.6
  38.9 5.8 %copy-done.3 = bf16[8,4096,256]{2,1,0:T(8,128)(2,1)S(1)} copy-done((bf16[8,4096,256]{2,1,0:T(8,128)(2,1)S(1)}, bf16[8,4096,256]{2,1,0:T(8,128)(2,1)}, u32[]{:S(2)}) %copy-start.3) | copy-done | bytes 16777240
  44.6 17.9 %pack_columns.1 = bf16[8,16,32,1024]{3,2,1,0:T(8,128)(2,1)S(1)} custom-call(s32[16,128]{1,0:T(8,128)S(1)} %get-tuple-element.17.first_ref, s32[16,128]{1,0:T(8,128)S(1)} %get-tuple-element.18.count_ref, s32[1]{0:T(128)} %bitcast.3.dev_ref, s32[128,256]{1,0:T(8,128)S(1)} %get-tuple-element.15.slots_ref, s32[8,32,128]{2,1,0:T(8,128)S(1)} %get-tuple-element.19.table_ref, ...), custom_call_target="tpu_custom_call" | custom-call | flops 12884901888 | bytes 25165824 | tf_op jit(solution)/shard_map/pack_columns/pallas_call | solution.py:198
  62.6 3.2 %copy-done = bf16[8,16,32,1024]{3,2,1,0:T(8,128)(2,1)} copy-done((bf16[8,16,32,1024]{3,2,1,0:T(8,128)(2,1)}, bf16[8,16,32,1024]{3,2,1,0:T(8,128)(2,1)S(1)}, u32[]{:S(2)}) %copy-start) | copy-done | bytes 8388632
  65.8 16.0 %all-to-all-start = ((bf16[128,32,1024]{2,1,0:T(8,128)(2,1)}), bf16[128,32,1024]{2,1,0:T(8,128)(2,1)}, u32[]{:S(2)}, u32[]{:S(2)}) async-start(bf16[128,32,1024]{2,1,0:T(8,128)(2,1)} %bitcast.26), calls=%async_computation | async-start | bytes 16777216 | tf_op jit(solution)/shard_map/all_to_all | solution.py:371
  81.9 0.6 all-gather.4.cloned.1.call-update
  82.5 128.3 %all-to-all-done.got_ref = bf16[128,32,1024]{2,1,0:T(8,128)(2,1)} async-done(((bf16[128,32,1024]{2,1,0:T(8,128)(2,1)}), bf16[128,32,1024]{2,1,0:T(8,128)(2,1)}, u32[]{:S(2)}, u32[]{:S(2)}) %all-to-all-start) | async-done | bytes 8388640 | tf_op jit(solution)/shard_map/all_to_all | solution.py:371
  210.8 16.2 %squeeze_and_first_shares.1 = (bf16[2048,1024]{1,0:T(8,128)(2,1)S(1)}, f32[2,512,512]{2,1,0:T(8,128)S(1)}, f32[2,512,512]{2,1,0:T(8,128)S(1)}) custom-call(s32[2]{0:T(128)S(1)} %pad_add_fusion.pos_ref, s32[16,128]{1,0:T(8,128)S(1)} %get-tuple-element.17.first_ref, s32[16,128]{1,0:T(8,128)S(1)} %get-tuple-element.18.count_ref, ...), custom_call_target="tpu_custom_call" | custom-call | flops 25769803776 | bytes 25165824 | tf_op jit(solution)/shard_map/squeeze_and_first_shares/pallas_call | solution.py:287
  227.0 0.9 collective-permute-start.2
  227.9 5.7 %next_shares.1 = (f32[2,512,512]{2,1,0:T(8,128)S(1)}, f32[2,512,512]{2,1,0:T(8,128)S(1)}) custom-call(s32[2]{0:T(128)S(1)} %pad_add_fusion.pos_ref, bf16[16,256,1024]{2,1,0:T(8,128)(2,1)S(1)} %bitcast.28, bf16[2048,1024]{1,0:T(8,128)(2,1)S(1)} %get-tuple-element.22.tile_ref), custom_call_target="tpu_custom_call" | custom-call | flops 12884901888 | bytes 16777216 | tf_op jit(solution)/shard_map/next_shares/pallas_call | solution.py:311
  233.7 0.5 add_convert_fusion
  234.3 1.0 slice_bitcast_fusion.2
  235.3 4.8 %collective-permute-start.3 = (bf16[512,512]{1,0:T(8,128)(2,1)}, bf16[512,512]{1,0:T(8,128)(2,1)S(1)}, u32[]{:S(2)}, u32[]{:S(2)}) collective-permute-start(bf16[512,512]{1,0:T(8,128)(2,1)} %get-tuple-element.34), channel_id=1, source_target_pairs={{0,64},{1,65},{2,66},{3,67},{4,68},{5,69},{6,70},{7,71},{8,72},{9,... | collective-permute-start | bytes 1572872 | tf_op jit(solution)/shard_map/ppermute | solution.py:380
  240.5 0.5 add.51
  241.0 3.0 collective-permute-start.5
  244.0 9.1 %collective-permute-done.3 = bf16[512,512]{1,0:T(8,128)(2,1)S(1)} collective-permute-done((bf16[512,512]{1,0:T(8,128)(2,1)}, bf16[512,512]{1,0:T(8,128)(2,1)S(1)}, u32[]{:S(2)}, u32[]{:S(2)}) %collective-permute-start.3) | collective-permute-done | bytes 524320 | tf_op jit(solution)/shard_map/ppermute | solution.py:380
  253.1 10.7 %collective-permute-done.4 = bf16[512,512]{1,0:T(8,128)(2,1)} collective-permute-done((bf16[512,512]{1,0:T(8,128)(2,1)}, bf16[512,512]{1,0:T(8,128)(2,1)}, u32[]{:S(2)}, u32[]{:S(2)}) %collective-permute-start.4) | collective-permute-done | bytes 524320 | tf_op jit(solution)/shard_map/ppermute | solution.py:380
  263.9 1.6 fusion.13
  265.7 1.9 collective-permute-done.6
  267.8 4.7 %convolution_convert_fusion = bf16[2048,256]{1,0:T(8,128)(2,1)} fusion(bf16[2048,1024]{1,0:T(8,128)(2,1)} %all-gather.4.cloned.1.call-done, f32[256,512]{1,0:T(8,128)S(1)} %get-tuple-element.33, f32[256,512]{1,0:T(8,128)S(1)} %get-tuple-element.32), kind=kOutput, calls=%fused_computation.5 | convolution fusion | flops 1075314688 | bytes 6291456 | tf_op jit(solution)/shard_map/dot_general | solution.py:20
  272.5 11.5 %all-to-all-start.1 = ((bf16[16,128,256]{2,1,0:T(8,128)(2,1)}), bf16[16,128,256]{2,1,0:T(8,128)(2,1)S(1)}, u32[]{:S(2)}, u32[]{:S(2)}) async-start(bf16[16,128,256]{2,1,0:T(8,128)(2,1)} %bitcast.9), calls=%async_computation.1 | async-start | bytes 2097152 | tf_op jit(solution)/shard_map/all_to_all | solution.py:394
  284.1 2.2 fusion
  286.3 2.0 fusion.7
  288.3 13.5 %all-to-all-done.1 = bf16[16,128,256]{2,1,0:T(8,128)(2,1)S(1)} async-done(((bf16[16,128,256]{2,1,0:T(8,128)(2,1)}), bf16[16,128,256]{2,1,0:T(8,128)(2,1)S(1)}, u32[]{:S(2)}, u32[]{:S(2)}) %all-to-all-start.1) | async-done | bytes 1048608 | tf_op jit(solution)/shard_map/all_to_all | solution.py:394
  301.9 0.8 copy.10
  (39 shorter events, 1.4 us)
Async XLA Ops:
  7.2 203.7 %all-gather.6.cloned.1.call-start = ((), (), s32[]{:S(2)}) async-start(), calls=%async_computation.3 | async-start | bytes 8912896 | tf_op jit(solution)/shard_map/all_gather | solution.py:366
  8.5 5.4 %copy-start.10 = (s32[16384]{0:T(1024)S(1)}, s32[16384]{0:T(1024)}, u32[]{:S(2)}) copy-start(s32[16384]{0:T(1024)} %param.6) | copy-start | bytes 196612
  13.1 10.5 %copy-start.5 = (bf16[256,1024]{1,0:T(8,128)(2,1)}, bf16[256,1024]{1,0:T(8,128)(2,1)S(1)}, u32[]{:S(2)}) copy-start(bf16[256,1024]{1,0:T(8,128)(2,1)S(1)} %fusion.8) | copy-start | bytes 1572868
  13.1 24.9 %collective-permute-start = (bf16[256,1024]{1,0:T(8,128)(2,1)S(1)}, bf16[256,1024]{1,0:T(8,128)(2,1)S(1)}, u32[]{:S(2)}, u32[]{:S(2)}) collective-permute-start(bf16[256,1024]{1,0:T(8,128)(2,1)S(1)} %fusion.8), channel_id=1, source_target_pairs={{0,0},{1,2},{2,16},{3,18},{4,32},{5,34},{6,48},{7,50},{8,64},{9,66... | collective-permute-start | bytes 1572872 | tf_op jit(solution)/shard_map/ppermute | solution.py:360
  32.3 5.7 %copy-start.2 = (bf16[8,4096,256]{2,1,0:T(8,128)(2,1)}, bf16[8,4096,256]{2,1,0:T(8,128)(2,1)S(1)}, u32[]{:S(2)}) copy-start(bf16[8,4096,256]{2,1,0:T(8,128)(2,1)S(1)} %sort_columns.1.data_ref) | copy-start | bytes 50331652
  38.0 0.8 copy-start.6
  38.9 5.8 %copy-start.3 = (bf16[8,4096,256]{2,1,0:T(8,128)(2,1)S(1)}, bf16[8,4096,256]{2,1,0:T(8,128)(2,1)}, u32[]{:S(2)}) copy-start(bf16[8,4096,256]{2,1,0:T(8,128)(2,1)} %copy-done.2) | copy-start | bytes 50331652
  62.5 3.2 %copy-start = (bf16[8,16,32,1024]{3,2,1,0:T(8,128)(2,1)}, bf16[8,16,32,1024]{3,2,1,0:T(8,128)(2,1)S(1)}, u32[]{:S(2)}) copy-start(bf16[8,16,32,1024]{3,2,1,0:T(8,128)(2,1)S(1)} %pack_columns.1) | copy-start | bytes 25165828
  65.8 145.0 %all-to-all-start = ((bf16[128,32,1024]{2,1,0:T(8,128)(2,1)}), bf16[128,32,1024]{2,1,0:T(8,128)(2,1)}, u32[]{:S(2)}, u32[]{:S(2)}) async-start(bf16[128,32,1024]{2,1,0:T(8,128)(2,1)} %bitcast.26), calls=%async_computation | async-start | bytes 16777216 | tf_op jit(solution)/shard_map/all_to_all | solution.py:371
  81.8 186.0 %all-gather.4.cloned.1.call-start = ((), (), s32[]{:S(2)}) async-start(), calls=%async_computation.2 | async-start | bytes 4718592 | tf_op jit(solution)/shard_map/all_gather | solution.py:369
  210.8 17.1 %copy-start.1 = (bf16[4096,1024]{1,0:T(8,128)(2,1)S(1)}, bf16[4096,1024]{1,0:T(8,128)(2,1)}, u32[]{:S(2)}) copy-start(bf16[4096,1024]{1,0:T(8,128)(2,1)} %all-gather.6.cloned.1.call-done) | copy-start | bytes 25165828
  227.0 6.7 %collective-permute-start.2 = (f32[2,512,512]{2,1,0:T(8,128)S(1)}, f32[2,512,512]{2,1,0:T(8,128)S(1)}, u32[]{:S(2)}, u32[]{:S(2)}) collective-permute-start(f32[2,512,512]{2,1,0:T(8,128)S(1)} %get-tuple-element.26), channel_id=1, source_target_pairs={{0,16},{1,17},{2,18},{3,19},{4,20},{5,21},{6,22},{7,23},{8,24},{9,... | collective-permute-start | bytes 6291464 | tf_op jit(solution)/shard_map/ppermute | solution.py:375
  233.6 6.9 %collective-permute-start.1 = (f32[2,512,512]{2,1,0:T(8,128)S(1)}, f32[2,512,512]{2,1,0:T(8,128)S(1)}, u32[]{:S(2)}, u32[]{:S(2)}) collective-permute-start(f32[2,512,512]{2,1,0:T(8,128)S(1)} %get-tuple-element.24), channel_id=1, source_target_pairs={{0,16},{1,17},{2,18},{3,19},{4,20},{5,21},{6,22},{7,23},{8,24},{9,... | collective-permute-start | bytes 6291464 | tf_op jit(solution)/shard_map/ppermute | solution.py:377
  235.3 17.8 %collective-permute-start.3 = (bf16[512,512]{1,0:T(8,128)(2,1)}, bf16[512,512]{1,0:T(8,128)(2,1)S(1)}, u32[]{:S(2)}, u32[]{:S(2)}) collective-permute-start(bf16[512,512]{1,0:T(8,128)(2,1)} %get-tuple-element.34), channel_id=1, source_target_pairs={{0,64},{1,65},{2,66},{3,67},{4,68},{5,69},{6,70},{7,71},{8,72},{9,... | collective-permute-start | bytes 1572872 | tf_op jit(solution)/shard_map/ppermute | solution.py:380
  240.2 23.7 %collective-permute-start.4 = (bf16[512,512]{1,0:T(8,128)(2,1)}, bf16[512,512]{1,0:T(8,128)(2,1)}, u32[]{:S(2)}, u32[]{:S(2)}) collective-permute-start(bf16[512,512]{1,0:T(8,128)(2,1)} %get-tuple-element.35), channel_id=1, source_target_pairs={{0,32},{1,33},{2,34},{3,35},{4,36},{5,37},{6,38},{7,39},{8,40},{9,... | collective-permute-start | bytes 1572872 | tf_op jit(solution)/shard_map/ppermute | solution.py:380
  241.0 22.9 %collective-permute-start.5 = (bf16[512,512]{1,0:T(8,128)(2,1)S(1)}, bf16[512,512]{1,0:T(8,128)(2,1)}, u32[]{:S(2)}, u32[]{:S(2)}) collective-permute-start(bf16[512,512]{1,0:T(8,128)(2,1)S(1)} %fusion.18), channel_id=1, source_target_pairs={{0,96},{1,97},{2,98},{3,99},{4,100},{5,101},{6,102},{7,103},{8,104... | collective-permute-start | bytes 1572872 | tf_op jit(solution)/shard_map/ppermute | solution.py:380
  253.1 10.7 %copy-start.4 = (bf16[512,512]{1,0:T(8,128)(2,1)}, bf16[512,512]{1,0:T(8,128)(2,1)S(1)}, u32[]{:S(2)}) copy-start(bf16[512,512]{1,0:T(8,128)(2,1)S(1)} %collective-permute-done.3) | copy-start | bytes 1572868
  265.6 2.0 collective-permute-start.6
  267.7 4.7 %copy-start.7 = (f32[256,512]{1,0:T(8,128)}, f32[256,512]{1,0:T(8,128)S(1)}, u32[]{:S(2)}) copy-start(f32[256,512]{1,0:T(8,128)S(1)} %get-tuple-element.33) | copy-start | bytes 1572868
  267.8 16.2 %copy-start.9 = (f32[256,128]{1,0:T(8,128)S(1)}, f32[256,128]{1,0:T(8,128)}, u32[]{:S(2)}) copy-start(f32[256,128]{1,0:T(8,128)} %param.9) | copy-start | bytes 393220
  272.5 29.3 %all-to-all-start.1 = ((bf16[16,128,256]{2,1,0:T(8,128)(2,1)}), bf16[16,128,256]{2,1,0:T(8,128)(2,1)S(1)}, u32[]{:S(2)}, u32[]{:S(2)}) async-start(bf16[16,128,256]{2,1,0:T(8,128)(2,1)} %bitcast.9), calls=%async_computation.1 | async-start | bytes 2097152 | tf_op jit(solution)/shard_map/all_to_all | solution.py:394
  284.0 2.3 copy-start.8
Sparse Core Ops, SparseCore 0:
  39.0 161.6 all-gather.5
  202.4 37.9 all-gather.3

commit v2 on v0

--- a/solution.py
+++ b/solution.py
@@ -121,7 +121,7 @@
             out_ref[b, k * SLOT:(k + 1) * SLOT, :] = part[b * SLOT:(b + 1) * SLOT]
 
 
-def sort_columns(cov, slots, blocks, per_step=16):
+def sort_columns(cov, slots, blocks, per_step=32):
     rows, width = cov.shape
     ranges, cols = slots.shape
     return pl.pallas_call(
@@ -163,7 +163,14 @@
 
         return lax.fori_loop(1, count_ref[tile, w], more, carry)
 
-    lax.fori_loop(0, group * windows, extra, 0)
+    most = count_ref[block * group, 0]
+    for job in range(1, group * windows):
+        most = jnp.maximum(most, count_ref[block * group + job // windows, job % windows])
+
+    @pl.when(most > 1)
+    def _():
+        lax.fori_loop(0, group * windows, extra, 0)
+
     for g in range(group):
         out = dot_nt(rows_hot, acc[g * width:(g + 1) * width, :]).astype(BF)
         for b in range(blocks):
@@ -277,7 +284,7 @@
         functools.partial(first_kernel, steps),
         in_specs=[smem, smem, smem, vmem, hbm, hbm],
         out_specs=(vmem, vmem, vmem),
-        out_shape=(jax.ShapeDtypeStruct((depth, cols), BF), share, share),
+        out_shape=(pltpu.VMEM((depth, cols), BF), share, share),
         scratch_shapes=[
             pltpu.VMEM((owners, SLOT, cols), BF),
             pltpu.VMEM((len(steps), rows, depth), BF),
@@ -285,6 +292,7 @@
             pltpu.SemaphoreType.DMA((len(steps), 4)),
         ],
         cost_estimate=pl.CostEstimate(flops=24 << 30, bytes_accessed=24 << 20, transcendentals=0),
+        compiler_params=pltpu.CompilerParams(vmem_limit_bytes=36 << 20),
         name="squeeze_and_first_shares",
     )(position, firsts, counts, table, received, u_block)
 
@@ -306,6 +314,7 @@
             pltpu.SemaphoreType.DMA((len(steps), 4)),
         ],
         cost_estimate=pl.CostEstimate(flops=12 << 30, bytes_accessed=16 << 20, transcendentals=0),
+        compiler_params=pltpu.CompilerParams(vmem_limit_bytes=24 << 20),
         name="next_shares",
     )(position, u_block, tile)
 

time: 309 us -> 300 us (0.971)
  Pallas kernels: 77.8 us -> 67.5 us
  starting transfers between devices: 26.4 us -> 29.9 us
    pallas_call x1, Pallas kernels: 10.1 us -> 5.68 us  [next_shares(): pl.pallas_call(functools.partial(next_kernel, steps), in_specs=[smem, hbm...]
  transfers between devices with their start and end apart: 11 -> 11, of which waited for: 5 -> 5; matrix products, arithmetic and copies ran while one was open for 4% -> 3% of each run, Pallas kernels for 25% -> 23%
where the time goes in v2:
time: 300 us; the launch traced here: 299 us
  waiting for transfers between devices  166 us (55%)
  Pallas kernels  67.5 us (22%)
  starting transfers between devices  29.9 us (10%)
  between operations  14.3 us (5%)
  matrix products  13.5 us (4%)
  local copies, waits for them, and re-layouts  4.19 us (1%)
  other arithmetic  3.6 us (1%)
    all_to_all x1, waiting for transfers between devices, local(): lax.all_to_all(flat_out, both, split_axis=0, concat_axis=0, tiled=True)  129 us
    pallas_call x1, Pallas kernels, pack_columns(): pl.pallas_call(pack_kernel, grid_spec=grid_spec, out_shape=jax.ShapeDtype...  21.3 us
    ppermute x3, waiting for transfers between devices, local(): lax.ppermute(share, both, pairs(lambda z, core, y, x, step=step: ((z + st...  20.9 us
    pallas_call x1, Pallas kernels, first_shares(): pl.pallas_call(functools.partial(first_kernel, steps), in_specs=[smem, sm...  16.2 us
    all_to_all x1, starting transfers between devices, local(): lax.all_to_all(flat_out, both, split_axis=0, concat_axis=0, tiled=True)  15.1 us
    all_to_all x1, waiting for transfers between devices, local(): lax.all_to_all(ss_part, 'col', split_axis=0, concat_axis=0, tiled=True)  13.5 us
    pallas_call x1, Pallas kernels, sort_columns(): pl.pallas_call(functools.partial(sort_kernel, per_step), grid=(ranges //...  13.2 us
    pallas_call x1, Pallas kernels, index_tables(): pl.pallas_call(functools.partial(index_kernel, tiles), out_shape=(jax.Sha...  11.2 us
  transfers between devices with their start and end apart: 11, of which 5 were waited for; matrix products, arithmetic and copies ran while one was open for 3% of the time, Pallas kernels for 23%

profile of v2, /device:TPU:0, one launch (start us, length us, event | category | flops | bytes accessed | tf_op | source)
XLA Modules:
  0.0 298.9 jit_solution(13233196393783274106)
XLA Ops:
  7.2 0.7 dynamic_slice.9
  7.9 0.6 convert_reduce_fusion
  8.5 4.6 %fusion.8 = bf16[256,1024]{1,0:T(8,128)(2,1)S(1)} fusion(s32[1024]{0:T(1024)S(1)} %convert_reduce_fusion, bf16[1024,2048]{1,0:T(8,128)(2,1)} %param.7, bf16[2048,256]{1,0:T(8,128)(2,1)} %param.8, s32[256]{0:T(256)S(1)} %iota_add_fusion), kind=kOutput, calls=%fused_computation.14 | convolution fusion | flops 1613234176 | bytes 5772288 | tf_op jit(solution)/shard_map/dot_general | solution.py:353
  13.1 0.7 collective-permute-start
  13.8 0.6 reshape.29.anc_ref
  14.5 11.2 %index_tables.1 = (s32[128,256]{1,0:T(8,128)}, s32[8,32,128]{2,1,0:T(8,128)}, s32[16,128]{1,0:T(8,128)}, s32[16,128]{1,0:T(8,128)}) custom-call(s32[8,2048]{1,0:T(8,128)} %reshape.29.anc_ref), custom_call_target="tpu_custom_call" | custom-call | flops 8589934592 | bytes 1048576 | tf_op jit(solution)/shard_map/index_tables/pallas_call | solution.py:88
  25.7 13.2 %sort_columns.1.data_ref = bf16[8,4096,256]{2,1,0:T(8,128)(2,1)} custom-call(s32[128,256]{1,0:T(8,128)} %get-tuple-element.15.slots_ref, bf16[256,32768]{1,0:T(8,128)(2,1)} %cov_ref.1), custom_call_target="tpu_custom_call" | custom-call | flops 12884901888 | bytes 33554432 | tf_op jit(solution)/shard_map/sort_columns/pallas_call | solution.py:127
  38.9 0.8 copy-done.6
  39.7 21.3 %pack_columns.1 = bf16[8,16,32,1024]{3,2,1,0:T(8,128)(2,1)} custom-call(s32[16,128]{1,0:T(8,128)} %get-tuple-element.17.first_ref, s32[16,128]{1,0:T(8,128)} %get-tuple-element.18.count_ref, s32[1]{0:T(128)} %bitcast.3.dev_ref, s32[128,256]{1,0:T(8,128)} %get-tuple-element.15.slots_ref, s32[8,32,128]{2,1,0:T(8,128)} %get-tuple-element.19.table_ref, ...), custom_call_target="tpu_custom_call" | custom-call | flops 12884901888 | bytes 25165824 | tf_op jit(solution)/shard_map/pack_columns/pallas_call | solution.py:195
  61.0 15.1 %all-to-all-start = ((bf16[128,32,1024]{2,1,0:T(8,128)(2,1)}), bf16[128,32,1024]{2,1,0:T(8,128)(2,1)}, u32[]{:S(2)}, u32[]{:S(2)}) async-start(bf16[128,32,1024]{2,1,0:T(8,128)(2,1)} %bitcast.28), calls=%async_computation | async-start | bytes 16777216 | tf_op jit(solution)/shard_map/all_to_all | solution.py:367
  76.3 0.6 all-gather.4.cloned.1.call-update
  76.9 128.9 %all-to-all-done.got_ref = bf16[128,32,1024]{2,1,0:T(8,128)(2,1)} async-done(((bf16[128,32,1024]{2,1,0:T(8,128)(2,1)}), bf16[128,32,1024]{2,1,0:T(8,128)(2,1)}, u32[]{:S(2)}, u32[]{:S(2)}) %all-to-all-start) | async-done | bytes 8388640 | tf_op jit(solution)/shard_map/all_to_all | solution.py:367
  205.8 16.2 %squeeze_and_first_shares.1 = (bf16[2048,1024]{1,0:T(8,128)(2,1)S(1)}, f32[2,512,512]{2,1,0:T(8,128)S(1)}, f32[2,512,512]{2,1,0:T(8,128)S(1)}) custom-call(s32[2]{0:T(128)S(1)} %pad_add_fusion.pos_ref, s32[16,128]{1,0:T(8,128)S(1)} %copy-done.2, s32[16,128]{1,0:T(8,128)S(1)} %copy-done.3, s32[8,32,128]{2,1,0:T(8,128)S(1)} %copy-done.1, ...), custom_call_target="tpu_custom_call" | custom-call | flops 25769803776 | bytes 25165824 | tf_op jit(solution)/shard_map/squeeze_and_first_shares/pallas_call | solution.py:283
  222.0 0.4 collective-permute-start.2
  222.4 5.7 %next_shares.1 = (f32[2,512,512]{2,1,0:T(8,128)S(1)}, f32[2,512,512]{2,1,0:T(8,128)S(1)}) custom-call(s32[2]{0:T(128)S(1)} %pad_add_fusion.pos_ref, bf16[16,256,1024]{2,1,0:T(8,128)(2,1)S(1)} %bitcast.27, bf16[2048,1024]{1,0:T(8,128)(2,1)S(1)} %get-tuple-element.22.tile_ref), custom_call_target="tpu_custom_call" | custom-call | flops 12884901888 | bytes 16777216 | tf_op jit(solution)/shard_map/next_shares/pallas_call | solution.py:307
  228.1 0.3 collective-permute-start.1
  228.4 0.5 add_convert_fusion
  228.9 1.0 slice_bitcast_fusion.2
  230.0 2.4 collective-permute-start.3
  232.4 0.5 add.51
  233.0 3.3 %collective-permute-start.5 = (bf16[512,512]{1,0:T(8,128)(2,1)S(1)}, bf16[512,512]{1,0:T(8,128)(2,1)}, u32[]{:S(2)}, u32[]{:S(2)}) collective-permute-start(bf16[512,512]{1,0:T(8,128)(2,1)S(1)} %fusion.18), channel_id=1, source_target_pairs={{0,96},{1,97},{2,98},{3,99},{4,100},{5,101},{6,102},{7,103},{8,104... | collective-permute-start | bytes 1572872 | tf_op jit(solution)/shard_map/ppermute | solution.py:376
  236.3 10.3 %collective-permute-done.3 = bf16[512,512]{1,0:T(8,128)(2,1)S(1)} collective-permute-done((bf16[512,512]{1,0:T(8,128)(2,1)}, bf16[512,512]{1,0:T(8,128)(2,1)S(1)}, u32[]{:S(2)}, u32[]{:S(2)}) %collective-permute-start.3) | collective-permute-done | bytes 524320 | tf_op jit(solution)/shard_map/ppermute | solution.py:376
  246.5 10.6 %collective-permute-done.4 = bf16[512,512]{1,0:T(8,128)(2,1)} collective-permute-done((bf16[512,512]{1,0:T(8,128)(2,1)}, bf16[512,512]{1,0:T(8,128)(2,1)}, u32[]{:S(2)}, u32[]{:S(2)}) %collective-permute-start.4) | collective-permute-done | bytes 524320 | tf_op jit(solution)/shard_map/ppermute | solution.py:376
  257.2 1.6 fusion.13
  259.0 1.9 collective-permute-done.6
  260.8 0.1 dynamic-slice_select_fusion.1
  261.1 4.7 %convolution_convert_fusion = bf16[2048,256]{1,0:T(8,128)(2,1)} fusion(bf16[2048,1024]{1,0:T(8,128)(2,1)} %all-gather.4.cloned.1.call-done, f32[256,512]{1,0:T(8,128)S(1)} %get-tuple-element.33, f32[256,512]{1,0:T(8,128)S(1)} %get-tuple-element.32), kind=kOutput, calls=%fused_computation.5 | convolution fusion | flops 1075314688 | bytes 6291456 | tf_op jit(solution)/shard_map/dot_general | solution.py:20
  265.7 7.6 %all-to-all-start.1 = ((bf16[16,128,256]{2,1,0:T(8,128)(2,1)}), bf16[16,128,256]{2,1,0:T(8,128)(2,1)S(1)}, u32[]{:S(2)}, u32[]{:S(2)}) async-start(bf16[16,128,256]{2,1,0:T(8,128)(2,1)} %bitcast.9), calls=%async_computation.1 | async-start | bytes 2097152 | tf_op jit(solution)/shard_map/all_to_all | solution.py:390
  273.4 2.2 fusion
  275.6 2.0 fusion.7
  277.6 13.5 %all-to-all-done.1 = bf16[16,128,256]{2,1,0:T(8,128)(2,1)S(1)} async-done(((bf16[16,128,256]{2,1,0:T(8,128)(2,1)}), bf16[16,128,256]{2,1,0:T(8,128)(2,1)S(1)}, u32[]{:S(2)}, u32[]{:S(2)}) %all-to-all-start.1) | async-done | bytes 1048608 | tf_op jit(solution)/shard_map/all_to_all | solution.py:390
  291.3 0.8 copy.10
  (39 shorter events, 0.7 us)
Async XLA Ops:
  7.2 198.7 %all-gather.6.cloned.1.call-start = ((), (), s32[]{:S(2)}) async-start(), calls=%async_computation.3 | async-start | bytes 8912896 | tf_op jit(solution)/shard_map/all_gather | solution.py:362
  8.5 5.4 %copy-start.10 = (s32[16384]{0:T(1024)S(1)}, s32[16384]{0:T(1024)}, u32[]{:S(2)}) copy-start(s32[16384]{0:T(1024)} %param.6) | copy-start | bytes 196612
  13.1 12.6 %copy-start.5 = (bf16[256,1024]{1,0:T(8,128)(2,1)}, bf16[256,1024]{1,0:T(8,128)(2,1)S(1)}, u32[]{:S(2)}) copy-start(bf16[256,1024]{1,0:T(8,128)(2,1)S(1)} %fusion.8) | copy-start | bytes 1572868
  13.1 25.8 %collective-permute-start = (bf16[256,1024]{1,0:T(8,128)(2,1)S(1)}, bf16[256,1024]{1,0:T(8,128)(2,1)S(1)}, u32[]{:S(2)}, u32[]{:S(2)}) collective-permute-start(bf16[256,1024]{1,0:T(8,128)(2,1)S(1)} %fusion.8), channel_id=1, source_target_pairs={{0,0},{1,2},{2,16},{3,18},{4,32},{5,34},{6,48},{7,50},{8,64},{9,66... | collective-permute-start | bytes 1572872 | tf_op jit(solution)/shard_map/ppermute | solution.py:356
  38.9 0.8 copy-start.6
  61.0 144.8 %copy-start.1 = (s32[8,32,128]{2,1,0:T(8,128)S(1)}, s32[8,32,128]{2,1,0:T(8,128)}, u32[]{:S(2)}) copy-start(s32[8,32,128]{2,1,0:T(8,128)} %get-tuple-element.19.table_ref) | copy-start | bytes 393220
  61.0 144.8 %copy-start.2 = (s32[16,128]{1,0:T(8,128)S(1)}, s32[16,128]{1,0:T(8,128)}, u32[]{:S(2)}) copy-start(s32[16,128]{1,0:T(8,128)} %get-tuple-element.17.first_ref) | copy-start | bytes 24580
  61.0 144.8 %copy-start.3 = (s32[16,128]{1,0:T(8,128)S(1)}, s32[16,128]{1,0:T(8,128)}, u32[]{:S(2)}) copy-start(s32[16,128]{1,0:T(8,128)} %get-tuple-element.18.count_ref) | copy-start | bytes 24580
  61.0 144.8 %all-to-all-start = ((bf16[128,32,1024]{2,1,0:T(8,128)(2,1)}), bf16[128,32,1024]{2,1,0:T(8,128)(2,1)}, u32[]{:S(2)}, u32[]{:S(2)}) async-start(bf16[128,32,1024]{2,1,0:T(8,128)(2,1)} %bitcast.28), calls=%async_computation | async-start | bytes 16777216 | tf_op jit(solution)/shard_map/all_to_all | solution.py:367
  76.1 184.9 %all-gather.4.cloned.1.call-start = ((), (), s32[]{:S(2)}) async-start(), calls=%async_computation.2 | async-start | bytes 4718592 | tf_op jit(solution)/shard_map/all_gather | solution.py:365
  205.8 16.6 %copy-start = (bf16[4096,1024]{1,0:T(8,128)(2,1)S(1)}, bf16[4096,1024]{1,0:T(8,128)(2,1)}, u32[]{:S(2)}) copy-start(bf16[4096,1024]{1,0:T(8,128)(2,1)} %all-gather.6.cloned.1.call-done) | copy-start | bytes 25165828
  222.0 6.4 %collective-permute-start.2 = (f32[2,512,512]{2,1,0:T(8,128)S(1)}, f32[2,512,512]{2,1,0:T(8,128)S(1)}, u32[]{:S(2)}, u32[]{:S(2)}) collective-permute-start(f32[2,512,512]{2,1,0:T(8,128)S(1)} %get-tuple-element.26), channel_id=1, source_target_pairs={{0,16},{1,17},{2,18},{3,19},{4,20},{5,21},{6,22},{7,23},{8,24},{9,... | collective-permute-start | bytes 6291464 | tf_op jit(solution)/shard_map/ppermute | solution.py:371
  228.1 4.3 %collective-permute-start.1 = (f32[2,512,512]{2,1,0:T(8,128)S(1)}, f32[2,512,512]{2,1,0:T(8,128)S(1)}, u32[]{:S(2)}, u32[]{:S(2)}) collective-permute-start(f32[2,512,512]{2,1,0:T(8,128)S(1)} %get-tuple-element.24), channel_id=1, source_target_pairs={{0,16},{1,17},{2,18},{3,19},{4,20},{5,21},{6,22},{7,23},{8,24},{9,... | collective-permute-start | bytes 6291464 | tf_op jit(solution)/shard_map/ppermute | solution.py:373
  230.0 16.5 %collective-permute-start.3 = (bf16[512,512]{1,0:T(8,128)(2,1)}, bf16[512,512]{1,0:T(8,128)(2,1)S(1)}, u32[]{:S(2)}, u32[]{:S(2)}) collective-permute-start(bf16[512,512]{1,0:T(8,128)(2,1)} %get-tuple-element.34), channel_id=1, source_target_pairs={{0,64},{1,65},{2,66},{3,67},{4,68},{5,69},{6,70},{7,71},{8,72},{9,... | collective-permute-start | bytes 1572872 | tf_op jit(solution)/shard_map/ppermute | solution.py:376
  232.4 24.8 %collective-permute-start.4 = (bf16[512,512]{1,0:T(8,128)(2,1)}, bf16[512,512]{1,0:T(8,128)(2,1)}, u32[]{:S(2)}, u32[]{:S(2)}) collective-permute-start(bf16[512,512]{1,0:T(8,128)(2,1)} %get-tuple-element.35), channel_id=1, source_target_pairs={{0,32},{1,33},{2,34},{3,35},{4,36},{5,37},{6,38},{7,39},{8,40},{9,... | collective-permute-start | bytes 1572872 | tf_op jit(solution)/shard_map/ppermute | solution.py:376
  233.0 24.2 %collective-permute-start.5 = (bf16[512,512]{1,0:T(8,128)(2,1)S(1)}, bf16[512,512]{1,0:T(8,128)(2,1)}, u32[]{:S(2)}, u32[]{:S(2)}) collective-permute-start(bf16[512,512]{1,0:T(8,128)(2,1)S(1)} %fusion.18), channel_id=1, source_target_pairs={{0,96},{1,97},{2,98},{3,99},{4,100},{5,101},{6,102},{7,103},{8,104... | collective-permute-start | bytes 1572872 | tf_op jit(solution)/shard_map/ppermute | solution.py:376
  246.5 10.7 %copy-start.4 = (bf16[512,512]{1,0:T(8,128)(2,1)}, bf16[512,512]{1,0:T(8,128)(2,1)S(1)}, u32[]{:S(2)}) copy-start(bf16[512,512]{1,0:T(8,128)(2,1)S(1)} %collective-permute-done.3) | copy-start | bytes 1572868
  258.9 2.0 collective-permute-start.6
  261.0 4.7 %copy-start.7 = (f32[256,512]{1,0:T(8,128)}, f32[256,512]{1,0:T(8,128)S(1)}, u32[]{:S(2)}) copy-start(f32[256,512]{1,0:T(8,128)S(1)} %get-tuple-element.33) | copy-start | bytes 1572868
  261.0 12.3 %copy-start.9 = (f32[256,128]{1,0:T(8,128)S(1)}, f32[256,128]{1,0:T(8,128)}, u32[]{:S(2)}) copy-start(f32[256,128]{1,0:T(8,128)} %param.9) | copy-start | bytes 393220
  265.7 25.4 %all-to-all-start.1 = ((bf16[16,128,256]{2,1,0:T(8,128)(2,1)}), bf16[16,128,256]{2,1,0:T(8,128)(2,1)S(1)}, u32[]{:S(2)}, u32[]{:S(2)}) async-start(bf16[16,128,256]{2,1,0:T(8,128)(2,1)} %bitcast.9), calls=%async_computation.1 | async-start | bytes 2097152 | tf_op jit(solution)/shard_map/all_to_all | solution.py:390
  273.3 2.3 copy-start.8
Sparse Core Ops, SparseCore 0:
  39.8 156.6 all-gather.5
  198.3 37.0 all-gather.3

commit v3 on v2

--- a/solution.py
+++ b/solution.py
@@ -52,35 +52,43 @@
     spread = iota((owners, LANES), 0) % per_line == iota((owners, LANES), 1) // SLOT
     s = (iota((lines, LANES), 1) % SLOT).astype(F32)
     edge = (iota((owners, LANES), 1) * WIN).astype(F32)
-    expand = lambda v: dot(pick, jnp.where(spread, v, 0.0).astype(BF))
+    spread = jnp.concatenate([spread] * tiles, axis=1)
+    edge = jnp.concatenate([edge] * tiles, axis=1)
+
+    def expand(v):
+        return dot(pick, jnp.where(spread, v, 0.0).astype(BF))
+
+    masks = [tile_of == float(c + 1) for c in range(tiles)]
+    both = dot(jnp.concatenate([ones_where(mask) for mask in masks], axis=0), before)
+    ahead = [both[c * owners:(c + 1) * owners, :rows] for c in range(tiles)]
+    numbers = [both[c * owners:(c + 1) * owners, rows:] for c in range(tiles)]
     slots = jnp.zeros((owners, rows), F32) - 1.0
+    for c in range(tiles):
+        lift = ahead[c] + float(c // 2 * SLOT + 1)
+        if c % 2:
+            lift = lift + jnp.concatenate([numbers[c - 1]] * (rows // LANES), axis=1)
+        slots = slots + jnp.where(masks[c], lift, 0.0)
+    slots_ref[...] = slots.astype(I32)
+    number = jnp.concatenate(numbers, axis=1)
+    start = dot(below, number.astype(BF))
+    end = start + number
+    lead = jnp.sum(jnp.where(end <= edge, 1.0, 0.0), axis=0, keepdims=True).astype(I32)
+    last = jnp.sum(jnp.where(start < edge + float(WIN), 1.0, 0.0), axis=0, keepdims=True).astype(I32) - 1
+    first = lead // per_line
+    count = (last // per_line - first) // REACH + 1
+    high = jnp.floor(start * (1.0 / 32.0))
+    n = expand(number)
+    p = expand(high) * 32.0 + expand(start - high * 32.0)
     tile_len = float(anc_ref.shape[0] * chunk // tiles)
-    prev = None
     for c in range(tiles):
-        mask = tile_of == float(c + 1)
-        both = dot(ones_where(mask), before)
-        ahead, number = both[:, :rows], both[:, rows:]
-        start = dot(below, number.astype(BF))
-        base = float(c // 2 * SLOT + 1)
-        lift = ahead + base
+        at = slice(c * LANES, (c + 1) * LANES)
+        first_ref[c:c + 1, :] = first[:, at]
+        count_ref[c:c + 1, :] = count[:, at]
         if c % 2:
-            lift = lift + jnp.concatenate([prev[0]] * (rows // LANES), axis=1)
-        slots = slots + jnp.where(mask, lift, 0.0)
-        high = jnp.floor(start * (1.0 / 32.0))
-        n = expand(number)
-        p = expand(high) * 32.0 + expand(start - high * 32.0)
-        end = start + number
-        lead = jnp.sum(jnp.where(end <= edge, 1.0, 0.0), axis=0, keepdims=True).astype(I32)
-        last = jnp.sum(jnp.where(start < edge + float(WIN), 1.0, 0.0), axis=0, keepdims=True).astype(I32) - 1
-        first = lead // per_line
-        first_ref[c:c + 1, :] = first
-        count_ref[c:c + 1, :] = (last // per_line - first) // REACH + 1
-        if c % 2:
-            n0, p0 = prev[1], prev[2]
-            to = jnp.where(s < n0, p0 + s, jnp.where(s < n0 + n, tile_len + p + s - n0, -1.0))
+            old = slice((c - 1) * LANES, c * LANES)
+            n0, p0 = n[:, old], p[:, old]
+            to = jnp.where(s < n0, p0 + s, jnp.where(s < n0 + n[:, at], tile_len + p[:, at] + s - n0, -1.0))
             table_ref[c // 2, 0:lines, :] = to.astype(I32)
-        prev = (number, n, p)
-    slots_ref[...] = slots.astype(I32)
 
 
 def index_tables(anc, owners, rows, tiles):
@@ -226,11 +234,16 @@
     half = keep_ref.shape[2]
     give = pl.multiple_of((1 - core) * half, half)
     keep = pl.multiple_of(core * half, half)
-    for n, copies in enumerate(jobs):
+    for copies in jobs:
         for copy in copies:
             copy.wait()
+
+    def product(n, carry):
         give_ref[n] = dot(lhs[n], tile_ref[:, pl.ds(give, half)])
         keep_ref[n] = dot(lhs[n], tile_ref[:, pl.ds(keep, half)])
+        return carry
+
+    lax.fori_loop(0, len(jobs), product, 0)
 
 
 def first_kernel(steps, pos_ref, first_ref, count_ref, table_ref, got_ref, u_ref,

time: 300 us -> 300 us (level)
  Pallas kernels: 67.5 us -> 62.2 us
  starting transfers between devices: 29.9 us -> 33.5 us
    all_to_all x1, starting transfers between devices: 15.1 us -> 19.6 us  [local(): lax.all_to_all(flat_out, both, split_axis=0, concat_axis=0, tiled=True)]
    pallas_call x1, Pallas kernels: 11.2 us -> 6.85 us  [index_tables(): pl.pallas_call(functools.partial(index_kernel, tiles), out_shape=(jax.Sha...]
  transfers between devices with their start and end apart: 11 -> 11, of which waited for: 5 -> 6; matrix products, arithmetic and copies ran while one was open for 3% -> 3% of each run, Pallas kernels for 23% -> 21%
where the time goes in v3:
time: 300 us; the launch traced here: 299 us
  waiting for transfers between devices  168 us (56%)
  Pallas kernels  62.2 us (21%)
  starting transfers between devices  33.5 us (11%)
  between operations  14.3 us (5%)
  matrix products  13.4 us (4%)
  local copies, waits for them, and re-layouts  4.19 us (1%)
  other arithmetic  3.6 us (1%)
    all_to_all x1, waiting for transfers between devices, local(): lax.all_to_all(flat_out, both, split_axis=0, concat_axis=0, tiled=True)  129 us
    ppermute x3, waiting for transfers between devices, local(): lax.ppermute(share, both, pairs(lambda z, core, y, x, step=step: ((z + st...  22.5 us
    pallas_call x1, Pallas kernels, pack_columns(): pl.pallas_call(pack_kernel, grid_spec=grid_spec, out_shape=jax.ShapeDtype...  20.4 us
    all_to_all x1, starting transfers between devices, local(): lax.all_to_all(flat_out, both, split_axis=0, concat_axis=0, tiled=True)  19.6 us
    pallas_call x1, Pallas kernels, first_shares(): pl.pallas_call(functools.partial(first_kernel, steps), in_specs=[smem, sm...  16.2 us
    all_to_all x1, waiting for transfers between devices, local(): lax.all_to_all(ss_part, 'col', split_axis=0, concat_axis=0, tiled=True)  13.6 us
    pallas_call x1, Pallas kernels, sort_columns(): pl.pallas_call(functools.partial(sort_kernel, per_step), grid=(ranges //...  13.2 us
    all_to_all x1, starting transfers between devices, local(): lax.all_to_all(ss_part, 'col', split_axis=0, concat_axis=0, tiled=True)  7.84 us
  transfers between devices with their start and end apart: 11, of which 6 were waited for; matrix products, arithmetic and copies ran while one was open for 3% of the time, Pallas kernels for 21%

profile of v3, /device:TPU:0, one launch (start us, length us, event | category | flops | bytes accessed | tf_op | source)
XLA Modules:
  0.0 299.3 jit_solution(10273669581956263307)
XLA Ops:
  7.2 0.7 dynamic_slice.9
  7.9 0.6 convert_reduce_fusion
  8.5 4.6 %fusion.8 = bf16[256,1024]{1,0:T(8,128)(2,1)S(1)} fusion(s32[1024]{0:T(1024)S(1)} %convert_reduce_fusion, bf16[1024,2048]{1,0:T(8,128)(2,1)} %param.7, bf16[2048,256]{1,0:T(8,128)(2,1)} %param.8, s32[256]{0:T(256)S(1)} %iota_add_fusion), kind=kOutput, calls=%fused_computation.14 | convolution fusion | flops 1613234176 | bytes 5772288 | tf_op jit(solution)/shard_map/dot_general | solution.py:366
  13.1 0.7 collective-permute-start
  13.8 0.6 reshape.29.anc_ref
  14.5 6.9 %index_tables.1 = (s32[128,256]{1,0:T(8,128)}, s32[8,32,128]{2,1,0:T(8,128)}, s32[16,128]{1,0:T(8,128)}, s32[16,128]{1,0:T(8,128)}) custom-call(s32[8,2048]{1,0:T(8,128)} %reshape.29.anc_ref), custom_call_target="tpu_custom_call" | custom-call | flops 8589934592 | bytes 1048576 | tf_op jit(solution)/shard_map/index_tables/pallas_call | solution.py:96
  21.3 13.2 %sort_columns.1.data_ref = bf16[8,4096,256]{2,1,0:T(8,128)(2,1)} custom-call(s32[128,256]{1,0:T(8,128)} %get-tuple-element.15.slots_ref, bf16[256,32768]{1,0:T(8,128)(2,1)} %cov_ref.1), custom_call_target="tpu_custom_call" | custom-call | flops 12884901888 | bytes 33554432 | tf_op jit(solution)/shard_map/sort_columns/pallas_call | solution.py:135
  34.5 0.8 copy-done.6
  35.4 20.4 %pack_columns.1 = bf16[8,16,32,1024]{3,2,1,0:T(8,128)(2,1)} custom-call(s32[16,128]{1,0:T(8,128)} %get-tuple-element.17.first_ref, s32[16,128]{1,0:T(8,128)} %get-tuple-element.18.count_ref, s32[1]{0:T(128)} %bitcast.3.dev_ref, s32[128,256]{1,0:T(8,128)} %get-tuple-element.15.slots_ref, s32[8,32,128]{2,1,0:T(8,128)} %get-tuple-element.19.table_ref, ...), custom_call_target="tpu_custom_call" | custom-call | flops 12884901888 | bytes 25165824 | tf_op jit(solution)/shard_map/pack_columns/pallas_call | solution.py:203
  55.7 19.6 %all-to-all-start = ((bf16[128,32,1024]{2,1,0:T(8,128)(2,1)}), bf16[128,32,1024]{2,1,0:T(8,128)(2,1)}, u32[]{:S(2)}, u32[]{:S(2)}) async-start(bf16[128,32,1024]{2,1,0:T(8,128)(2,1)} %bitcast.28), calls=%async_computation | async-start | bytes 16777216 | tf_op jit(solution)/shard_map/all_to_all | solution.py:380
  75.7 0.4 all-gather.4.cloned.1.call-update
  76.1 128.9 %all-to-all-done.got_ref = bf16[128,32,1024]{2,1,0:T(8,128)(2,1)} async-done(((bf16[128,32,1024]{2,1,0:T(8,128)(2,1)}), bf16[128,32,1024]{2,1,0:T(8,128)(2,1)}, u32[]{:S(2)}, u32[]{:S(2)}) %all-to-all-start) | async-done | bytes 8388640 | tf_op jit(solution)/shard_map/all_to_all | solution.py:380
  205.0 16.2 %squeeze_and_first_shares.1 = (bf16[2048,1024]{1,0:T(8,128)(2,1)S(1)}, f32[2,512,512]{2,1,0:T(8,128)S(1)}, f32[2,512,512]{2,1,0:T(8,128)S(1)}) custom-call(s32[2]{0:T(128)S(1)} %pad_add_fusion.pos_ref, s32[16,128]{1,0:T(8,128)S(1)} %copy-done.2, s32[16,128]{1,0:T(8,128)S(1)} %copy-done.3, s32[8,32,128]{2,1,0:T(8,128)S(1)} %copy-done.1, ...), custom_call_target="tpu_custom_call" | custom-call | flops 25769803776 | bytes 25165824 | tf_op jit(solution)/shard_map/squeeze_and_first_shares/pallas_call | solution.py:296
  221.2 1.2 collective-permute-start.2
  222.5 5.7 %next_shares.1 = (f32[2,512,512]{2,1,0:T(8,128)S(1)}, f32[2,512,512]{2,1,0:T(8,128)S(1)}) custom-call(s32[2]{0:T(128)S(1)} %pad_add_fusion.pos_ref, bf16[16,256,1024]{2,1,0:T(8,128)(2,1)S(1)} %bitcast.27, bf16[2048,1024]{1,0:T(8,128)(2,1)S(1)} %get-tuple-element.22.tile_ref), custom_call_target="tpu_custom_call" | custom-call | flops 12884901888 | bytes 16777216 | tf_op jit(solution)/shard_map/next_shares/pallas_call | solution.py:320
  228.3 0.5 add_convert_fusion
  228.8 1.0 slice_bitcast_fusion.2
  229.9 0.9 collective-permute-start.3
  230.8 0.8 collective-permute-start.4
  231.6 0.8 collective-permute-done.1
  232.4 0.5 add.51
  232.9 1.7 collective-permute-start.5
  234.7 11.7 %collective-permute-done.3 = bf16[512,512]{1,0:T(8,128)(2,1)S(1)} collective-permute-done((bf16[512,512]{1,0:T(8,128)(2,1)}, bf16[512,512]{1,0:T(8,128)(2,1)S(1)}, u32[]{:S(2)}, u32[]{:S(2)}) %collective-permute-start.3) | collective-permute-done | bytes 524320 | tf_op jit(solution)/shard_map/ppermute | solution.py:389
  246.4 10.8 %collective-permute-done.4 = bf16[512,512]{1,0:T(8,128)(2,1)} collective-permute-done((bf16[512,512]{1,0:T(8,128)(2,1)}, bf16[512,512]{1,0:T(8,128)(2,1)}, u32[]{:S(2)}, u32[]{:S(2)}) %collective-permute-start.4) | collective-permute-done | bytes 524320 | tf_op jit(solution)/shard_map/ppermute | solution.py:389
  257.1 1.6 fusion.13
  259.2 1.9 collective-permute-done.6
  261.2 4.7 %convolution_convert_fusion = bf16[2048,256]{1,0:T(8,128)(2,1)} fusion(bf16[2048,1024]{1,0:T(8,128)(2,1)} %all-gather.4.cloned.1.call-done, f32[256,512]{1,0:T(8,128)S(1)} %get-tuple-element.33, f32[256,512]{1,0:T(8,128)S(1)} %get-tuple-element.32), kind=kOutput, calls=%fused_computation.5 | convolution fusion | flops 1075314688 | bytes 6291456 | tf_op jit(solution)/shard_map/dot_general | solution.py:20
  265.9 7.8 %all-to-all-start.1 = ((bf16[16,128,256]{2,1,0:T(8,128)(2,1)}), bf16[16,128,256]{2,1,0:T(8,128)(2,1)S(1)}, u32[]{:S(2)}, u32[]{:S(2)}) async-start(bf16[16,128,256]{2,1,0:T(8,128)(2,1)} %bitcast.9), calls=%async_computation.1 | async-start | bytes 2097152 | tf_op jit(solution)/shard_map/all_to_all | solution.py:403
  273.9 2.1 fusion
  276.0 2.0 fusion.7
  278.0 13.6 %all-to-all-done.1 = bf16[16,128,256]{2,1,0:T(8,128)(2,1)S(1)} async-done(((bf16[16,128,256]{2,1,0:T(8,128)(2,1)}), bf16[16,128,256]{2,1,0:T(8,128)(2,1)S(1)}, u32[]{:S(2)}, u32[]{:S(2)}) %all-to-all-start.1) | async-done | bytes 1048608 | tf_op jit(solution)/shard_map/all_to_all | solution.py:403
  291.7 0.8 copy.10
  (39 shorter events, 1.4 us)
Async XLA Ops:
  7.2 197.8 %all-gather.6.cloned.1.call-start = ((), (), s32[]{:S(2)}) async-start(), calls=%async_computation.3 | async-start | bytes 8912896 | tf_op jit(solution)/shard_map/all_gather | solution.py:375
  8.5 5.4 %copy-start.10 = (s32[16384]{0:T(1024)S(1)}, s32[16384]{0:T(1024)}, u32[]{:S(2)}) copy-start(s32[16384]{0:T(1024)} %param.6) | copy-start | bytes 196612
  13.1 8.2 %copy-start.5 = (bf16[256,1024]{1,0:T(8,128)(2,1)}, bf16[256,1024]{1,0:T(8,128)(2,1)S(1)}, u32[]{:S(2)}) copy-start(bf16[256,1024]{1,0:T(8,128)(2,1)S(1)} %fusion.8) | copy-start | bytes 1572868
  13.1 21.4 %collective-permute-start = (bf16[256,1024]{1,0:T(8,128)(2,1)S(1)}, bf16[256,1024]{1,0:T(8,128)(2,1)S(1)}, u32[]{:S(2)}, u32[]{:S(2)}) collective-permute-start(bf16[256,1024]{1,0:T(8,128)(2,1)S(1)} %fusion.8), channel_id=1, source_target_pairs={{0,0},{1,2},{2,16},{3,18},{4,32},{5,34},{6,48},{7,50},{8,64},{9,66... | collective-permute-start | bytes 1572872 | tf_op jit(solution)/shard_map/ppermute | solution.py:369
  34.5 0.8 copy-start.6
  55.7 149.3 %copy-start.1 = (s32[8,32,128]{2,1,0:T(8,128)S(1)}, s32[8,32,128]{2,1,0:T(8,128)}, u32[]{:S(2)}) copy-start(s32[8,32,128]{2,1,0:T(8,128)} %get-tuple-element.19.table_ref) | copy-start | bytes 393220
  55.7 149.3 %copy-start.2 = (s32[16,128]{1,0:T(8,128)S(1)}, s32[16,128]{1,0:T(8,128)}, u32[]{:S(2)}) copy-start(s32[16,128]{1,0:T(8,128)} %get-tuple-element.17.first_ref) | copy-start | bytes 24580
  55.7 149.3 %copy-start.3 = (s32[16,128]{1,0:T(8,128)S(1)}, s32[16,128]{1,0:T(8,128)}, u32[]{:S(2)}) copy-start(s32[16,128]{1,0:T(8,128)} %get-tuple-element.18.count_ref) | copy-start | bytes 24580
  55.7 149.3 %all-to-all-start = ((bf16[128,32,1024]{2,1,0:T(8,128)(2,1)}), bf16[128,32,1024]{2,1,0:T(8,128)(2,1)}, u32[]{:S(2)}, u32[]{:S(2)}) async-start(bf16[128,32,1024]{2,1,0:T(8,128)(2,1)} %bitcast.28), calls=%async_computation | async-start | bytes 16777216 | tf_op jit(solution)/shard_map/all_to_all | solution.py:380
  75.3 185.9 %all-gather.4.cloned.1.call-start = ((), (), s32[]{:S(2)}) async-start(), calls=%async_computation.2 | async-start | bytes 4718592 | tf_op jit(solution)/shard_map/all_gather | solution.py:378
  205.0 17.4 %copy-start = (bf16[4096,1024]{1,0:T(8,128)(2,1)S(1)}, bf16[4096,1024]{1,0:T(8,128)(2,1)}, u32[]{:S(2)}) copy-start(bf16[4096,1024]{1,0:T(8,128)(2,1)} %all-gather.6.cloned.1.call-done) | copy-start | bytes 25165828
  221.2 7.1 %collective-permute-start.2 = (f32[2,512,512]{2,1,0:T(8,128)S(1)}, f32[2,512,512]{2,1,0:T(8,128)S(1)}, u32[]{:S(2)}, u32[]{:S(2)}) collective-permute-start(f32[2,512,512]{2,1,0:T(8,128)S(1)} %get-tuple-element.26), channel_id=1, source_target_pairs={{0,16},{1,17},{2,18},{3,19},{4,20},{5,21},{6,22},{7,23},{8,24},{9,... | collective-permute-start | bytes 6291464 | tf_op jit(solution)/shard_map/ppermute | solution.py:384
  228.2 4.2 %collective-permute-start.1 = (f32[2,512,512]{2,1,0:T(8,128)S(1)}, f32[2,512,512]{2,1,0:T(8,128)S(1)}, u32[]{:S(2)}, u32[]{:S(2)}) collective-permute-start(f32[2,512,512]{2,1,0:T(8,128)S(1)} %get-tuple-element.24), channel_id=1, source_target_pairs={{0,16},{1,17},{2,18},{3,19},{4,20},{5,21},{6,22},{7,23},{8,24},{9,... | collective-permute-start | bytes 6291464 | tf_op jit(solution)/shard_map/ppermute | solution.py:386
  229.9 16.5 %collective-permute-start.3 = (bf16[512,512]{1,0:T(8,128)(2,1)}, bf16[512,512]{1,0:T(8,128)(2,1)S(1)}, u32[]{:S(2)}, u32[]{:S(2)}) collective-permute-start(bf16[512,512]{1,0:T(8,128)(2,1)} %get-tuple-element.34), channel_id=1, source_target_pairs={{0,64},{1,65},{2,66},{3,67},{4,68},{5,69},{6,70},{7,71},{8,72},{9,... | collective-permute-start | bytes 1572872 | tf_op jit(solution)/shard_map/ppermute | solution.py:389
  230.8 26.3 %collective-permute-start.4 = (bf16[512,512]{1,0:T(8,128)(2,1)}, bf16[512,512]{1,0:T(8,128)(2,1)}, u32[]{:S(2)}, u32[]{:S(2)}) collective-permute-start(bf16[512,512]{1,0:T(8,128)(2,1)} %get-tuple-element.35), channel_id=1, source_target_pairs={{0,32},{1,33},{2,34},{3,35},{4,36},{5,37},{6,38},{7,39},{8,40},{9,... | collective-permute-start | bytes 1572872 | tf_op jit(solution)/shard_map/ppermute | solution.py:389
  232.9 24.2 %collective-permute-start.5 = (bf16[512,512]{1,0:T(8,128)(2,1)S(1)}, bf16[512,512]{1,0:T(8,128)(2,1)}, u32[]{:S(2)}, u32[]{:S(2)}) collective-permute-start(bf16[512,512]{1,0:T(8,128)(2,1)S(1)} %fusion.18), channel_id=1, source_target_pairs={{0,96},{1,97},{2,98},{3,99},{4,100},{5,101},{6,102},{7,103},{8,104... | collective-permute-start | bytes 1572872 | tf_op jit(solution)/shard_map/ppermute | solution.py:389
  246.4 10.8 %copy-start.4 = (bf16[512,512]{1,0:T(8,128)(2,1)}, bf16[512,512]{1,0:T(8,128)(2,1)S(1)}, u32[]{:S(2)}) copy-start(bf16[512,512]{1,0:T(8,128)(2,1)S(1)} %collective-permute-done.3) | copy-start | bytes 1572868
  258.8 2.2 collective-permute-start.6
  261.2 4.7 %copy-start.7 = (f32[256,512]{1,0:T(8,128)}, f32[256,512]{1,0:T(8,128)S(1)}, u32[]{:S(2)}) copy-start(f32[256,512]{1,0:T(8,128)S(1)} %get-tuple-element.33) | copy-start | bytes 1572868
  261.2 12.5 %copy-start.9 = (f32[256,128]{1,0:T(8,128)S(1)}, f32[256,128]{1,0:T(8,128)}, u32[]{:S(2)}) copy-start(f32[256,128]{1,0:T(8,128)} %param.9) | copy-start | bytes 393220
  265.9 25.6 %all-to-all-start.1 = ((bf16[16,128,256]{2,1,0:T(8,128)(2,1)}), bf16[16,128,256]{2,1,0:T(8,128)(2,1)S(1)}, u32[]{:S(2)}, u32[]{:S(2)}) async-start(bf16[16,128,256]{2,1,0:T(8,128)(2,1)} %bitcast.9), calls=%async_computation.1 | async-start | bytes 2097152 | tf_op jit(solution)/shard_map/all_to_all | solution.py:403
  273.8 2.2 copy-start.8
Sparse Core Ops, SparseCore 0:
  35.5 160.6 all-gather.5
  197.9 36.8 all-gather.3

commit v4 on v3

--- a/solution.py
+++ b/solution.py
@@ -374,8 +374,8 @@
     piece, data = lax.optimization_barrier((piece, data))
     u_block = lax.all_gather(piece, "col", axis=0)
     outgoing = pack_columns(data, slots, table, firsts, counts, device, tile_cols)
-    outgoing, u_t = lax.optimization_barrier((outgoing, u_t))
     u_cols = lax.all_gather(u_t, "row", axis=0, tiled=True)
+    outgoing, u_cols = lax.optimization_barrier((outgoing, u_cols))
     flat_out = outgoing.reshape(owners * SLOT, tile_cols)
     received = lax.all_to_all(flat_out, both, split_axis=0, concat_axis=0, tiled=True)
     received = received.reshape(owners, SLOT, tile_cols)

time: 300 us -> 314 us (1.047)
  waiting for transfers between devices: 168 us -> 174 us
  starting transfers between devices: 33.5 us -> 38.6 us
    all_gather x1, waiting for transfers between devices: 0.01 us -> 23.7 us  [local(): u_block = lax.all_gather(piece, 'col', axis=0)]
    all_to_all x1, waiting for transfers between devices: 129 us -> 112 us  [local(): lax.all_to_all(flat_out, both, split_axis=0, concat_axis=0, tiled=True)]
    ppermute x3, starting transfers between devices: 3.46 us -> 8.31 us  [local(): lax.ppermute(share, both, pairs(lambda z, core, y, x, step=step: ((z + st...]
  transfers between devices with their start and end apart: 11 -> 11, of which waited for: 6 -> 8; matrix products, arithmetic and copies ran while one was open for 3% -> 2% of each run, Pallas kernels for 21% -> 15%
where the time goes in v4:
time: 314 us; the launch traced here: 313 us
  waiting for transfers between devices  174 us (55%)
  Pallas kernels  63.4 us (20%)
  starting transfers between devices  38.6 us (12%)
  between operations  14.2 us (5%)
  matrix products  14 us (4%)
  local copies, waits for them, and re-layouts  4.97 us (2%)
  other arithmetic  3.55 us (1%)
    all_to_all x1, waiting for transfers between devices, local(): lax.all_to_all(flat_out, both, split_axis=0, concat_axis=0, tiled=True)  112 us
    all_gather x1, waiting for transfers between devices, local(): u_block = lax.all_gather(piece, 'col', axis=0)  23.7 us
    ppermute x3, waiting for transfers between devices, local(): lax.ppermute(share, both, pairs(lambda z, core, y, x, step=step: ((z + st...  21.5 us
    pallas_call x1, Pallas kernels, pack_columns(): pl.pallas_call(pack_kernel, grid_spec=grid_spec, out_shape=jax.ShapeDtype...  21.3 us
    all_to_all x1, starting transfers between devices, local(): lax.all_to_all(flat_out, both, split_axis=0, concat_axis=0, tiled=True)  17 us
    pallas_call x1, Pallas kernels, first_shares(): pl.pallas_call(functools.partial(first_kernel, steps), in_specs=[smem, sm...  16.2 us
    all_to_all x1, waiting for transfers between devices, local(): lax.all_to_all(ss_part, 'col', split_axis=0, concat_axis=0, tiled=True)  13.6 us
    pallas_call x1, Pallas kernels, sort_columns(): pl.pallas_call(functools.partial(sort_kernel, per_step), grid=(ranges //...  13.4 us
  transfers between devices with their start and end apart: 11, of which 8 were waited for; matrix products, arithmetic and copies ran while one was open for 2% of the time, Pallas kernels for 15%

profile of v4, /device:TPU:0, one launch (start us, length us, event | category | flops | bytes accessed | tf_op | source)
XLA Modules:
  0.0 313.0 jit_solution(12493130545120773841)
XLA Ops:
  7.2 0.7 dynamic_slice.9
  7.9 0.6 convert_reduce_fusion
  8.5 5.4 %fusion.8 = bf16[256,1024]{1,0:T(8,128)(2,1)} fusion(s32[1024]{0:T(1024)S(1)} %convert_reduce_fusion, bf16[1024,2048]{1,0:T(8,128)(2,1)} %param.7, bf16[2048,256]{1,0:T(8,128)(2,1)} %param.8, s32[256]{0:T(256)S(1)} %iota_add_fusion), kind=kOutput, calls=%fused_computation.14 | convolution fusion | flops 1613234176 | bytes 5772288 | tf_op jit(solution)/shard_map/dot_general | solution.py:366
  14.0 1.7 collective-permute-start
  15.7 0.7 reshape.29.anc_ref
  16.3 6.8 %index_tables.1 = (s32[128,256]{1,0:T(8,128)}, s32[8,32,128]{2,1,0:T(8,128)}, s32[16,128]{1,0:T(8,128)}, s32[16,128]{1,0:T(8,128)}) custom-call(s32[8,2048]{1,0:T(8,128)} %reshape.29.anc_ref), custom_call_target="tpu_custom_call" | custom-call | flops 8589934592 | bytes 1048576 | tf_op jit(solution)/shard_map/index_tables/pallas_call | solution.py:96
  23.2 13.4 %sort_columns.1.data_ref = bf16[8,4096,256]{2,1,0:T(8,128)(2,1)} custom-call(s32[128,256]{1,0:T(8,128)} %get-tuple-element.15.slots_ref, bf16[256,32768]{1,0:T(8,128)(2,1)} %cov_ref.1), custom_call_target="tpu_custom_call" | custom-call | flops 12884901888 | bytes 33554432 | tf_op jit(solution)/shard_map/sort_columns/pallas_call | solution.py:135
  36.6 0.8 copy-done.5
  37.5 21.3 %pack_columns.1 = bf16[8,16,32,1024]{3,2,1,0:T(8,128)(2,1)} custom-call(s32[16,128]{1,0:T(8,128)} %get-tuple-element.17.first_ref, s32[16,128]{1,0:T(8,128)} %get-tuple-element.18.count_ref, s32[1]{0:T(128)} %bitcast.3.dev_ref, s32[128,256]{1,0:T(8,128)} %get-tuple-element.15.slots_ref, s32[8,32,128]{2,1,0:T(8,128)} %get-tuple-element.19.table_ref, ...), custom_call_target="tpu_custom_call" | custom-call | flops 12884901888 | bytes 25165824 | tf_op jit(solution)/shard_map/pack_columns/pallas_call | solution.py:203
  58.7 1.9 all-gather.4.cloned.1.call-done
  60.6 17.0 %all-to-all-start = ((bf16[128,32,1024]{2,1,0:T(8,128)(2,1)}), bf16[128,32,1024]{2,1,0:T(8,128)(2,1)}, u32[]{:S(2)}, u32[]{:S(2)}) async-start(bf16[128,32,1024]{2,1,0:T(8,128)(2,1)} %bitcast.28), calls=%async_computation | async-start | bytes 16777216 | tf_op jit(solution)/shard_map/all_to_all | solution.py:380
  77.7 111.5 %all-to-all-done.got_ref = bf16[128,32,1024]{2,1,0:T(8,128)(2,1)} async-done(((bf16[128,32,1024]{2,1,0:T(8,128)(2,1)}), bf16[128,32,1024]{2,1,0:T(8,128)(2,1)}, u32[]{:S(2)}, u32[]{:S(2)}) %all-to-all-start) | async-done | bytes 8388640 | tf_op jit(solution)/shard_map/all_to_all | solution.py:380
  189.2 23.7 %all-gather.6.cloned.1.call-done = bf16[4096,1024]{1,0:T(8,128)(2,1)} async-done(((bf16[256,1024]{1,0:T(8,128)(2,1)}), bf16[4096,1024]{1,0:T(8,128)(2,1)}) %all-gather.6.cloned.1.call-update) | async-done | bytes 8388624 | tf_op jit(solution)/shard_map/all_gather | solution.py:375
  212.9 16.2 %squeeze_and_first_shares.1 = (bf16[2048,1024]{1,0:T(8,128)(2,1)S(1)}, f32[2,512,512]{2,1,0:T(8,128)S(1)}, f32[2,512,512]{2,1,0:T(8,128)S(1)}) custom-call(s32[2]{0:T(128)S(1)} %pad_add_fusion.pos_ref, s32[16,128]{1,0:T(8,128)S(1)} %copy-done.2, s32[16,128]{1,0:T(8,128)S(1)} %copy-done.3, s32[8,32,128]{2,1,0:T(8,128)S(1)} %copy-done.1, ...), custom_call_target="tpu_custom_call" | custom-call | flops 25769803776 | bytes 25165824 | tf_op jit(solution)/shard_map/squeeze_and_first_shares/pallas_call | solution.py:296
  229.2 5.7 %next_shares.1 = (f32[2,512,512]{2,1,0:T(8,128)S(1)}, f32[2,512,512]{2,1,0:T(8,128)S(1)}) custom-call(s32[2]{0:T(128)S(1)} %pad_add_fusion.pos_ref, bf16[16,256,1024]{2,1,0:T(8,128)(2,1)S(1)} %bitcast.27, bf16[2048,1024]{1,0:T(8,128)(2,1)S(1)} %get-tuple-element.22.tile_ref), custom_call_target="tpu_custom_call" | custom-call | flops 12884901888 | bytes 16777216 | tf_op jit(solution)/shard_map/next_shares/pallas_call | solution.py:320
  234.9 0.6 collective-permute-start.1
  236.1 1.0 slice_bitcast_fusion.2
  237.1 4.7 %collective-permute-start.3 = (bf16[512,512]{1,0:T(8,128)(2,1)}, bf16[512,512]{1,0:T(8,128)(2,1)S(1)}, u32[]{:S(2)}, u32[]{:S(2)}) collective-permute-start(bf16[512,512]{1,0:T(8,128)(2,1)} %get-tuple-element.34), channel_id=1, source_target_pairs={{0,64},{1,65},{2,66},{3,67},{4,68},{5,69},{6,70},{7,71},{8,72},{9,... | collective-permute-start | bytes 1572872 | tf_op jit(solution)/shard_map/ppermute | solution.py:389
  241.8 2.2 collective-permute-start.4
  244.6 1.4 collective-permute-start.5
  246.0 8.9 %collective-permute-done.3 = bf16[512,512]{1,0:T(8,128)(2,1)S(1)} collective-permute-done((bf16[512,512]{1,0:T(8,128)(2,1)}, bf16[512,512]{1,0:T(8,128)(2,1)S(1)}, u32[]{:S(2)}, u32[]{:S(2)}) %collective-permute-start.3) | collective-permute-done | bytes 524320 | tf_op jit(solution)/shard_map/ppermute | solution.py:389
  254.9 11.1 %collective-permute-done.4 = bf16[512,512]{1,0:T(8,128)(2,1)} collective-permute-done((bf16[512,512]{1,0:T(8,128)(2,1)}, bf16[512,512]{1,0:T(8,128)(2,1)}, u32[]{:S(2)}, u32[]{:S(2)}) %collective-permute-start.4) | collective-permute-done | bytes 524320 | tf_op jit(solution)/shard_map/ppermute | solution.py:389
  266.0 1.5 collective-permute-done.5
  267.5 1.6 fusion.13
  269.5 1.9 collective-permute-done.6
  271.5 0.8 copy-done.6
  272.3 4.6 %convolution_convert_fusion = bf16[2048,256]{1,0:T(8,128)(2,1)} fusion(bf16[2048,1024]{1,0:T(8,128)(2,1)} %all-gather.4.cloned.1.call-done, f32[256,512]{1,0:T(8,128)S(1)} %get-tuple-element.33, f32[256,512]{1,0:T(8,128)S(1)} %get-tuple-element.32), kind=kOutput, calls=%fused_computation.5 | convolution fusion | flops 1075314688 | bytes 6291456 | tf_op jit(solution)/shard_map/dot_general | solution.py:20
  276.8 10.6 %all-to-all-start.1 = ((bf16[16,128,256]{2,1,0:T(8,128)(2,1)}), bf16[16,128,256]{2,1,0:T(8,128)(2,1)S(1)}, u32[]{:S(2)}, u32[]{:S(2)}) async-start(bf16[16,128,256]{2,1,0:T(8,128)(2,1)} %bitcast.9), calls=%async_computation.1 | async-start | bytes 2097152 | tf_op jit(solution)/shard_map/all_to_all | solution.py:403
  287.5 2.1 fusion
  289.6 2.0 fusion.7
  291.6 13.6 %all-to-all-done.1 = bf16[16,128,256]{2,1,0:T(8,128)(2,1)S(1)} async-done(((bf16[16,128,256]{2,1,0:T(8,128)(2,1)}), bf16[16,128,256]{2,1,0:T(8,128)(2,1)S(1)}, u32[]{:S(2)}, u32[]{:S(2)}) %all-to-all-start.1) | async-done | bytes 1048608 | tf_op jit(solution)/shard_map/all_to_all | solution.py:403
  305.4 0.8 copy.10
  (37 shorter events, 2.1 us)
Async XLA Ops:
  7.2 53.5 %all-gather.4.cloned.1.call-start = ((), (), s32[]{:S(2)}) async-start(), calls=%async_computation.2 | async-start | bytes 4718592 | tf_op jit(solution)/shard_map/all_gather | solution.py:377
  8.5 7.2 %copy-start.9 = (s32[16384]{0:T(1024)S(1)}, s32[16384]{0:T(1024)}, u32[]{:S(2)}) copy-start(s32[16384]{0:T(1024)} %param.6) | copy-start | bytes 196612
  13.9 199.0 %all-gather.6.cloned.1.call-start = ((), (), s32[]{:S(2)}) async-start(), calls=%async_computation.3 | async-start | bytes 8912896 | tf_op jit(solution)/shard_map/all_gather | solution.py:375
  14.0 22.6 %collective-permute-start = (bf16[256,1024]{1,0:T(8,128)(2,1)}, bf16[256,1024]{1,0:T(8,128)(2,1)S(1)}, u32[]{:S(2)}, u32[]{:S(2)}) collective-permute-start(bf16[256,1024]{1,0:T(8,128)(2,1)} %fusion.8), channel_id=1, source_target_pairs={{0,0},{1,2},{2,16},{3,18},{4,32},{5,34},{6,48},{7,50},{8,64},{9,66... | collective-permute-start | bytes 1572872 | tf_op jit(solution)/shard_map/ppermute | solution.py:369
  36.6 0.8 copy-start.5
  60.6 152.3 %copy-start.1 = (s32[8,32,128]{2,1,0:T(8,128)S(1)}, s32[8,32,128]{2,1,0:T(8,128)}, u32[]{:S(2)}) copy-start(s32[8,32,128]{2,1,0:T(8,128)} %get-tuple-element.19.table_ref) | copy-start | bytes 393220
  60.6 152.3 %copy-start.2 = (s32[16,128]{1,0:T(8,128)S(1)}, s32[16,128]{1,0:T(8,128)}, u32[]{:S(2)}) copy-start(s32[16,128]{1,0:T(8,128)} %get-tuple-element.17.first_ref) | copy-start | bytes 24580
  60.6 152.3 %copy-start.3 = (s32[16,128]{1,0:T(8,128)S(1)}, s32[16,128]{1,0:T(8,128)}, u32[]{:S(2)}) copy-start(s32[16,128]{1,0:T(8,128)} %get-tuple-element.18.count_ref) | copy-start | bytes 24580
  60.6 128.6 %all-to-all-start = ((bf16[128,32,1024]{2,1,0:T(8,128)(2,1)}), bf16[128,32,1024]{2,1,0:T(8,128)(2,1)}, u32[]{:S(2)}, u32[]{:S(2)}) async-start(bf16[128,32,1024]{2,1,0:T(8,128)(2,1)} %bitcast.28), calls=%async_computation | async-start | bytes 16777216 | tf_op jit(solution)/shard_map/all_to_all | solution.py:380
  212.9 16.3 %copy-start = (bf16[4096,1024]{1,0:T(8,128)(2,1)S(1)}, bf16[4096,1024]{1,0:T(8,128)(2,1)}, u32[]{:S(2)}) copy-start(bf16[4096,1024]{1,0:T(8,128)(2,1)} %all-gather.6.cloned.1.call-done) | copy-start | bytes 25165828
  229.1 6.4 %collective-permute-start.2 = (f32[2,512,512]{2,1,0:T(8,128)S(1)}, f32[2,512,512]{2,1,0:T(8,128)S(1)}, u32[]{:S(2)}, u32[]{:S(2)}) collective-permute-start(f32[2,512,512]{2,1,0:T(8,128)S(1)} %get-tuple-element.26), channel_id=1, source_target_pairs={{0,16},{1,17},{2,18},{3,19},{4,20},{5,21},{6,22},{7,23},{8,24},{9,... | collective-permute-start | bytes 6291464 | tf_op jit(solution)/shard_map/ppermute | solution.py:384
  234.9 9.1 %collective-permute-start.1 = (f32[2,512,512]{2,1,0:T(8,128)S(1)}, f32[2,512,512]{2,1,0:T(8,128)S(1)}, u32[]{:S(2)}, u32[]{:S(2)}) collective-permute-start(f32[2,512,512]{2,1,0:T(8,128)S(1)} %get-tuple-element.24), channel_id=1, source_target_pairs={{0,16},{1,17},{2,18},{3,19},{4,20},{5,21},{6,22},{7,23},{8,24},{9,... | collective-permute-start | bytes 6291464 | tf_op jit(solution)/shard_map/ppermute | solution.py:386
  237.1 17.8 %collective-permute-start.3 = (bf16[512,512]{1,0:T(8,128)(2,1)}, bf16[512,512]{1,0:T(8,128)(2,1)S(1)}, u32[]{:S(2)}, u32[]{:S(2)}) collective-permute-start(bf16[512,512]{1,0:T(8,128)(2,1)} %get-tuple-element.34), channel_id=1, source_target_pairs={{0,64},{1,65},{2,66},{3,67},{4,68},{5,69},{6,70},{7,71},{8,72},{9,... | collective-permute-start | bytes 1572872 | tf_op jit(solution)/shard_map/ppermute | solution.py:389
  241.8 24.1 %collective-permute-start.4 = (bf16[512,512]{1,0:T(8,128)(2,1)}, bf16[512,512]{1,0:T(8,128)(2,1)}, u32[]{:S(2)}, u32[]{:S(2)}) collective-permute-start(bf16[512,512]{1,0:T(8,128)(2,1)} %get-tuple-element.35), channel_id=1, source_target_pairs={{0,32},{1,33},{2,34},{3,35},{4,36},{5,37},{6,38},{7,39},{8,40},{9,... | collective-permute-start | bytes 1572872 | tf_op jit(solution)/shard_map/ppermute | solution.py:389
  244.6 22.9 %collective-permute-start.5 = (bf16[512,512]{1,0:T(8,128)(2,1)S(1)}, bf16[512,512]{1,0:T(8,128)(2,1)}, u32[]{:S(2)}, u32[]{:S(2)}) collective-permute-start(bf16[512,512]{1,0:T(8,128)(2,1)S(1)} %fusion.18), channel_id=1, source_target_pairs={{0,96},{1,97},{2,98},{3,99},{4,100},{5,101},{6,102},{7,103},{8,104... | collective-permute-start | bytes 1572872 | tf_op jit(solution)/shard_map/ppermute | solution.py:389
  254.9 11.1 %copy-start.4 = (bf16[512,512]{1,0:T(8,128)(2,1)}, bf16[512,512]{1,0:T(8,128)(2,1)S(1)}, u32[]{:S(2)}) copy-start(bf16[512,512]{1,0:T(8,128)(2,1)S(1)} %collective-permute-done.3) | copy-start | bytes 1572868
  269.2 2.2 collective-permute-start.6
  271.5 0.8 copy-start.6
  272.3 15.1 %copy-start.8 = (f32[256,128]{1,0:T(8,128)S(1)}, f32[256,128]{1,0:T(8,128)}, u32[]{:S(2)}) copy-start(f32[256,128]{1,0:T(8,128)} %param.9) | copy-start | bytes 393220
  276.8 12.8 %copy-start.7 = (f32[256,512]{1,0:T(8,128)S(1)}, f32[256,512]{1,0:T(8,128)}, u32[]{:S(2)}) copy-start(f32[256,512]{1,0:T(8,128)} %copy-done.6) | copy-start | bytes 1572868
  276.8 28.4 %all-to-all-start.1 = ((bf16[16,128,256]{2,1,0:T(8,128)(2,1)}), bf16[16,128,256]{2,1,0:T(8,128)(2,1)S(1)}, u32[]{:S(2)}, u32[]{:S(2)}) async-start(bf16[16,128,256]{2,1,0:T(8,128)(2,1)} %bitcast.9), calls=%async_computation.1 | async-start | bytes 2097152 | tf_op jit(solution)/shard_map/all_to_all | solution.py:403
Sparse Core Ops, SparseCore 0:
  14.1 46.5 all-gather.3
  62.8 150.1 all-gather.5

commit v5 on v2

--- a/solution.py
+++ b/solution.py
@@ -229,7 +229,7 @@
     for n, copies in enumerate(jobs):
         for copy in copies:
             copy.wait()
-        give_ref[n] = dot(lhs[n], tile_ref[:, pl.ds(give, half)])
+        give_ref[n] = dot(lhs[n], tile_ref[:, pl.ds(give, half)]).astype(BF)
         keep_ref[n] = dot(lhs[n], tile_ref[:, pl.ds(keep, half)])
 
 
@@ -284,7 +284,7 @@
         functools.partial(first_kernel, steps),
         in_specs=[smem, smem, smem, vmem, hbm, hbm],
         out_specs=(vmem, vmem, vmem),
-        out_shape=(pltpu.VMEM((depth, cols), BF), share, share),
+        out_shape=(pltpu.VMEM((depth, cols), BF), share, jax.ShapeDtypeStruct(share.shape, BF)),
         scratch_shapes=[
             pltpu.VMEM((owners, SLOT, cols), BF),
             pltpu.VMEM((len(steps), rows, depth), BF),
@@ -308,7 +308,7 @@
         functools.partial(next_kernel, steps),
         in_specs=[smem, hbm, vmem],
         out_specs=(vmem, vmem),
-        out_shape=(share, share),
+        out_shape=(share, jax.ShapeDtypeStruct(share.shape, BF)),
         scratch_shapes=[
             pltpu.VMEM((len(steps), rows, depth), BF),
             pltpu.SemaphoreType.DMA((len(steps), 4)),
@@ -368,9 +368,9 @@
     received = received.reshape(owners, SLOT, tile_cols)
 
     tile, keep, give = first_shares((2, 1), position, firsts, counts, table, received, u_block)
-    first = (keep + lax.ppermute(give, both, swap)).astype(BF)
+    first = (keep + lax.ppermute(give, both, swap).astype(F32)).astype(BF)
     keep, give = next_shares((3, 0), position, u_block, tile)
-    second = keep + lax.ppermute(give, both, swap)
+    second = keep + lax.ppermute(give, both, swap).astype(F32)
     total = second[1]
     for step, share in ((2, first[0]), (1, first[1]), (3, second[0].astype(BF))):
         share = lax.ppermute(

time: 300 us -> 299 us (level)
  transfers between devices with their start and end apart: 11 -> 11, of which waited for: 5 -> 5; matrix products, arithmetic and copies ran while one was open for 3% -> 3% of each run, Pallas kernels for 23% -> 22%
where the time goes in v5:
time: 299 us
  waiting for transfers between devices  168 us (56%)
  Pallas kernels  66.6 us (22%)
  starting transfers between devices  29.5 us (10%)
  between operations  14.3 us (5%)
  matrix products  13.5 us (5%)
  local copies, waits for them, and re-layouts  4.19 us (1%)
  other arithmetic  3.31 us (1%)
    all_to_all x1, waiting for transfers between devices, local(): lax.all_to_all(flat_out, both, split_axis=0, concat_axis=0, tiled=True)  129 us
    ppermute x3, waiting for transfers between devices, local(): lax.ppermute(share, both, pairs(lambda z, core, y, x, step=step: ((z + st...  22.6 us
    pallas_call x1, Pallas kernels, pack_columns(): pl.pallas_call(pack_kernel, grid_spec=grid_spec, out_shape=jax.ShapeDtype...  20.4 us
    pallas_call x1, Pallas kernels, first_shares(): pl.pallas_call(functools.partial(first_kernel, steps), in_specs=[smem, sm...  16.2 us
    all_to_all x1, starting transfers between devices, local(): lax.all_to_all(flat_out, both, split_axis=0, concat_axis=0, tiled=True)  15.2 us
    all_to_all x1, waiting for transfers between devices, local(): lax.all_to_all(ss_part, 'col', split_axis=0, concat_axis=0, tiled=True)  13.5 us
    pallas_call x1, Pallas kernels, sort_columns(): pl.pallas_call(functools.partial(sort_kernel, per_step), grid=(ranges //...  13.2 us
    pallas_call x1, Pallas kernels, index_tables(): pl.pallas_call(functools.partial(index_kernel, tiles), out_shape=(jax.Sha...  11.2 us
  transfers between devices with their start and end apart: 11, of which 5 were waited for; matrix products, arithmetic and copies ran while one was open for 3% of the time, Pallas kernels for 22%

profile of v5, /device:TPU:0, one launch (start us, length us, event | category | flops | bytes accessed | tf_op | source)
XLA Modules:
  0.0 298.9 jit_solution(8407303634588680980)
XLA Ops:
  7.2 0.7 dynamic_slice.9
  7.9 0.6 convert_reduce_fusion
  8.5 4.6 %fusion.8 = bf16[256,1024]{1,0:T(8,128)(2,1)S(1)} fusion(s32[1024]{0:T(1024)S(1)} %convert_reduce_fusion, bf16[1024,2048]{1,0:T(8,128)(2,1)} %param.7, bf16[2048,256]{1,0:T(8,128)(2,1)} %param.8, s32[256]{0:T(256)S(1)} %iota_add_fusion), kind=kOutput, calls=%fused_computation.15 | convolution fusion | flops 1613234176 | bytes 5772288 | tf_op jit(solution)/shard_map/dot_general | solution.py:353
  13.1 0.7 collective-permute-start
  13.8 0.6 reshape.29.anc_ref
  14.5 11.2 %index_tables.1 = (s32[128,256]{1,0:T(8,128)}, s32[8,32,128]{2,1,0:T(8,128)}, s32[16,128]{1,0:T(8,128)}, s32[16,128]{1,0:T(8,128)}) custom-call(s32[8,2048]{1,0:T(8,128)} %reshape.29.anc_ref), custom_call_target="tpu_custom_call" | custom-call | flops 8589934592 | bytes 1048576 | tf_op jit(solution)/shard_map/index_tables/pallas_call | solution.py:88
  25.7 13.2 %sort_columns.1.data_ref = bf16[8,4096,256]{2,1,0:T(8,128)(2,1)} custom-call(s32[128,256]{1,0:T(8,128)} %get-tuple-element.15.slots_ref, bf16[256,32768]{1,0:T(8,128)(2,1)} %cov_ref.1), custom_call_target="tpu_custom_call" | custom-call | flops 12884901888 | bytes 33554432 | tf_op jit(solution)/shard_map/sort_columns/pallas_call | solution.py:127
  38.9 0.8 copy-done.6
  39.7 20.4 %pack_columns.1 = bf16[8,16,32,1024]{3,2,1,0:T(8,128)(2,1)} custom-call(s32[16,128]{1,0:T(8,128)} %get-tuple-element.17.first_ref, s32[16,128]{1,0:T(8,128)} %get-tuple-element.18.count_ref, s32[1]{0:T(128)} %bitcast.3.dev_ref, s32[128,256]{1,0:T(8,128)} %get-tuple-element.15.slots_ref, s32[8,32,128]{2,1,0:T(8,128)} %get-tuple-element.19.table_ref, ...), custom_call_target="tpu_custom_call" | custom-call | flops 12884901888 | bytes 25165824 | tf_op jit(solution)/shard_map/pack_columns/pallas_call | solution.py:195
  60.1 15.2 %all-to-all-start = ((bf16[128,32,1024]{2,1,0:T(8,128)(2,1)}), bf16[128,32,1024]{2,1,0:T(8,128)(2,1)}, u32[]{:S(2)}, u32[]{:S(2)}) async-start(bf16[128,32,1024]{2,1,0:T(8,128)(2,1)} %bitcast.28), calls=%async_computation | async-start | bytes 16777216 | tf_op jit(solution)/shard_map/all_to_all | solution.py:367
  75.4 0.7 all-gather.4.cloned.1.call-update
  76.2 128.8 %all-to-all-done.got_ref = bf16[128,32,1024]{2,1,0:T(8,128)(2,1)} async-done(((bf16[128,32,1024]{2,1,0:T(8,128)(2,1)}), bf16[128,32,1024]{2,1,0:T(8,128)(2,1)}, u32[]{:S(2)}, u32[]{:S(2)}) %all-to-all-start) | async-done | bytes 8388640 | tf_op jit(solution)/shard_map/all_to_all | solution.py:367
  205.0 16.2 %squeeze_and_first_shares.1 = (bf16[2048,1024]{1,0:T(8,128)(2,1)S(1)}, f32[2,512,512]{2,1,0:T(8,128)S(1)}, bf16[2,512,512]{2,1,0:T(8,128)(2,1)S(1)}) custom-call(s32[2]{0:T(128)S(1)} %pad_add_fusion.pos_ref, s32[16,128]{1,0:T(8,128)S(1)} %copy-done.2, s32[16,128]{1,0:T(8,128)S(1)} %copy-done.3, s32[8,32,128]{2,1,0:T(8,128)S(1)} %copy-done.1, ...), custom_call_target="tpu_custom_call" | custom-call | flops 25769803776 | bytes 25165824 | tf_op jit(solution)/shard_map/squeeze_and_first_shares/pallas_call | solution.py:283
  221.2 1.3 collective-permute-start.2
  222.5 5.7 %next_shares.1 = (f32[2,512,512]{2,1,0:T(8,128)S(1)}, bf16[2,512,512]{2,1,0:T(8,128)(2,1)S(1)}) custom-call(s32[2]{0:T(128)S(1)} %pad_add_fusion.pos_ref, bf16[16,256,1024]{2,1,0:T(8,128)(2,1)S(1)} %bitcast.27, bf16[2048,1024]{1,0:T(8,128)(2,1)S(1)} %get-tuple-element.22.tile_ref), custom_call_target="tpu_custom_call" | custom-call | flops 12884901888 | bytes 16777216 | tf_op jit(solution)/shard_map/next_shares/pallas_call | solution.py:307
  228.3 0.3 add_convert_fusion
  228.6 1.0 slice_bitcast_fusion.2
  229.7 0.9 collective-permute-start.3
  230.6 0.8 collective-permute-start.4
  231.4 0.4 convert_add_fusion
  231.9 2.5 collective-permute-start.5
  234.4 11.8 %collective-permute-done.3 = bf16[512,512]{1,0:T(8,128)(2,1)S(1)} collective-permute-done((bf16[512,512]{1,0:T(8,128)(2,1)}, bf16[512,512]{1,0:T(8,128)(2,1)S(1)}, u32[]{:S(2)}, u32[]{:S(2)}) %collective-permute-start.3) | collective-permute-done | bytes 524320 | tf_op jit(solution)/shard_map/ppermute | solution.py:376
  246.2 10.8 %collective-permute-done.4 = bf16[512,512]{1,0:T(8,128)(2,1)} collective-permute-done((bf16[512,512]{1,0:T(8,128)(2,1)}, bf16[512,512]{1,0:T(8,128)(2,1)}, u32[]{:S(2)}, u32[]{:S(2)}) %collective-permute-start.4) | collective-permute-done | bytes 524320 | tf_op jit(solution)/shard_map/ppermute | solution.py:376
  256.9 1.6 fusion.13
  258.7 1.9 collective-permute-done.6
  260.6 0.1 dynamic-slice_select_fusion.1
  260.8 4.7 %convolution_convert_fusion = bf16[2048,256]{1,0:T(8,128)(2,1)} fusion(bf16[2048,1024]{1,0:T(8,128)(2,1)} %all-gather.4.cloned.1.call-done, f32[256,512]{1,0:T(8,128)S(1)} %get-tuple-element.33, f32[256,512]{1,0:T(8,128)S(1)} %get-tuple-element.32), kind=kOutput, calls=%fused_computation.5 | convolution fusion | flops 1075314688 | bytes 6291456 | tf_op jit(solution)/shard_map/dot_general | solution.py:20
  265.5 7.9 %all-to-all-start.1 = ((bf16[16,128,256]{2,1,0:T(8,128)(2,1)}), bf16[16,128,256]{2,1,0:T(8,128)(2,1)S(1)}, u32[]{:S(2)}, u32[]{:S(2)}) async-start(bf16[16,128,256]{2,1,0:T(8,128)(2,1)} %bitcast.9), calls=%async_computation.1 | async-start | bytes 2097152 | tf_op jit(solution)/shard_map/all_to_all | solution.py:390
  273.5 2.2 fusion
  275.7 2.0 fusion.7
  277.7 13.5 %all-to-all-done.1 = bf16[16,128,256]{2,1,0:T(8,128)(2,1)S(1)} async-done(((bf16[16,128,256]{2,1,0:T(8,128)(2,1)}), bf16[16,128,256]{2,1,0:T(8,128)(2,1)S(1)}, u32[]{:S(2)}, u32[]{:S(2)}) %all-to-all-start.1) | async-done | bytes 1048608 | tf_op jit(solution)/shard_map/all_to_all | solution.py:390
  291.3 0.8 copy.10
  (39 shorter events, 0.8 us)
Async XLA Ops:
  7.2 197.8 %all-gather.6.cloned.1.call-start = ((), (), s32[]{:S(2)}) async-start(), calls=%async_computation.3 | async-start | bytes 8912896 | tf_op jit(solution)/shard_map/all_gather | solution.py:362
  8.5 5.4 %copy-start.10 = (s32[16384]{0:T(1024)S(1)}, s32[16384]{0:T(1024)}, u32[]{:S(2)}) copy-start(s32[16384]{0:T(1024)} %param.6) | copy-start | bytes 196612
  13.1 12.6 %copy-start.5 = (bf16[256,1024]{1,0:T(8,128)(2,1)}, bf16[256,1024]{1,0:T(8,128)(2,1)S(1)}, u32[]{:S(2)}) copy-start(bf16[256,1024]{1,0:T(8,128)(2,1)S(1)} %fusion.8) | copy-start | bytes 1572868
  13.1 25.8 %collective-permute-start = (bf16[256,1024]{1,0:T(8,128)(2,1)S(1)}, bf16[256,1024]{1,0:T(8,128)(2,1)S(1)}, u32[]{:S(2)}, u32[]{:S(2)}) collective-permute-start(bf16[256,1024]{1,0:T(8,128)(2,1)S(1)} %fusion.8), channel_id=1, source_target_pairs={{0,0},{1,2},{2,16},{3,18},{4,32},{5,34},{6,48},{7,50},{8,64},{9,66... | collective-permute-start | bytes 1572872 | tf_op jit(solution)/shard_map/ppermute | solution.py:356
  38.9 0.8 copy-start.6
  60.1 144.9 %copy-start.1 = (s32[8,32,128]{2,1,0:T(8,128)S(1)}, s32[8,32,128]{2,1,0:T(8,128)}, u32[]{:S(2)}) copy-start(s32[8,32,128]{2,1,0:T(8,128)} %get-tuple-element.19.table_ref) | copy-start | bytes 393220
  60.1 144.9 %copy-start.2 = (s32[16,128]{1,0:T(8,128)S(1)}, s32[16,128]{1,0:T(8,128)}, u32[]{:S(2)}) copy-start(s32[16,128]{1,0:T(8,128)} %get-tuple-element.17.first_ref) | copy-start | bytes 24580
  60.1 144.9 %copy-start.3 = (s32[16,128]{1,0:T(8,128)S(1)}, s32[16,128]{1,0:T(8,128)}, u32[]{:S(2)}) copy-start(s32[16,128]{1,0:T(8,128)} %get-tuple-element.18.count_ref) | copy-start | bytes 24580
  60.1 144.9 %all-to-all-start = ((bf16[128,32,1024]{2,1,0:T(8,128)(2,1)}), bf16[128,32,1024]{2,1,0:T(8,128)(2,1)}, u32[]{:S(2)}, u32[]{:S(2)}) async-start(bf16[128,32,1024]{2,1,0:T(8,128)(2,1)} %bitcast.28), calls=%async_computation | async-start | bytes 16777216 | tf_op jit(solution)/shard_map/all_to_all | solution.py:367
  75.3 185.5 %all-gather.4.cloned.1.call-start = ((), (), s32[]{:S(2)}) async-start(), calls=%async_computation.2 | async-start | bytes 4718592 | tf_op jit(solution)/shard_map/all_gather | solution.py:365
  205.0 17.4 %copy-start = (bf16[4096,1024]{1,0:T(8,128)(2,1)S(1)}, bf16[4096,1024]{1,0:T(8,128)(2,1)}, u32[]{:S(2)}) copy-start(bf16[4096,1024]{1,0:T(8,128)(2,1)} %all-gather.6.cloned.1.call-done) | copy-start | bytes 25165828
  221.2 7.1 %collective-permute-start.2 = (bf16[2,512,512]{2,1,0:T(8,128)(2,1)S(1)}, bf16[2,512,512]{2,1,0:T(8,128)(2,1)S(1)}, u32[]{:S(2)}, u32[]{:S(2)}) collective-permute-start(bf16[2,512,512]{2,1,0:T(8,128)(2,1)S(1)} %get-tuple-element.26), channel_id=1, source_target_pairs={{0,16},{1,17},{2,18},{3,19},{4,20},{5,21},{6,22},{7,23},{8,24},{9,... | collective-permute-start | bytes 3145736 | tf_op jit(solution)/shard_map/ppermute | solution.py:371
  228.2 3.3 %collective-permute-start.1 = (bf16[2,512,512]{2,1,0:T(8,128)(2,1)S(1)}, bf16[2,512,512]{2,1,0:T(8,128)(2,1)S(1)}, u32[]{:S(2)}, u32[]{:S(2)}) collective-permute-start(bf16[2,512,512]{2,1,0:T(8,128)(2,1)S(1)} %get-tuple-element.24), channel_id=1, source_target_pairs={{0,16},{1,17},{2,18},{3,19},{4,20},{5,21},{6,22},{7,23},{8,24},{9,... | collective-permute-start | bytes 3145736 | tf_op jit(solution)/shard_map/ppermute | solution.py:373
  229.7 16.5 %collective-permute-start.3 = (bf16[512,512]{1,0:T(8,128)(2,1)}, bf16[512,512]{1,0:T(8,128)(2,1)S(1)}, u32[]{:S(2)}, u32[]{:S(2)}) collective-permute-start(bf16[512,512]{1,0:T(8,128)(2,1)} %get-tuple-element.34), channel_id=1, source_target_pairs={{0,64},{1,65},{2,66},{3,67},{4,68},{5,69},{6,70},{7,71},{8,72},{9,... | collective-permute-start | bytes 1572872 | tf_op jit(solution)/shard_map/ppermute | solution.py:376
  230.6 26.3 %collective-permute-start.4 = (bf16[512,512]{1,0:T(8,128)(2,1)}, bf16[512,512]{1,0:T(8,128)(2,1)}, u32[]{:S(2)}, u32[]{:S(2)}) collective-permute-start(bf16[512,512]{1,0:T(8,128)(2,1)} %get-tuple-element.35), channel_id=1, source_target_pairs={{0,32},{1,33},{2,34},{3,35},{4,36},{5,37},{6,38},{7,39},{8,40},{9,... | collective-permute-start | bytes 1572872 | tf_op jit(solution)/shard_map/ppermute | solution.py:376
  231.9 25.0 %collective-permute-start.5 = (bf16[512,512]{1,0:T(8,128)(2,1)S(1)}, bf16[512,512]{1,0:T(8,128)(2,1)}, u32[]{:S(2)}, u32[]{:S(2)}) collective-permute-start(bf16[512,512]{1,0:T(8,128)(2,1)S(1)} %fusion.18), channel_id=1, source_target_pairs={{0,96},{1,97},{2,98},{3,99},{4,100},{5,101},{6,102},{7,103},{8,104... | collective-permute-start | bytes 1572872 | tf_op jit(solution)/shard_map/ppermute | solution.py:376
  246.2 10.8 %copy-start.4 = (bf16[512,512]{1,0:T(8,128)(2,1)}, bf16[512,512]{1,0:T(8,128)(2,1)S(1)}, u32[]{:S(2)}) copy-start(bf16[512,512]{1,0:T(8,128)(2,1)S(1)} %collective-permute-done.3) | copy-start | bytes 1572868
  258.6 2.0 collective-permute-start.6
  260.8 4.7 %copy-start.7 = (f32[256,512]{1,0:T(8,128)}, f32[256,512]{1,0:T(8,128)S(1)}, u32[]{:S(2)}) copy-start(f32[256,512]{1,0:T(8,128)S(1)} %get-tuple-element.33) | copy-start | bytes 1572868
  260.8 12.6 %copy-start.9 = (f32[256,128]{1,0:T(8,128)S(1)}, f32[256,128]{1,0:T(8,128)}, u32[]{:S(2)}) copy-start(f32[256,128]{1,0:T(8,128)} %param.9) | copy-start | bytes 393220
  265.5 25.7 %all-to-all-start.1 = ((bf16[16,128,256]{2,1,0:T(8,128)(2,1)}), bf16[16,128,256]{2,1,0:T(8,128)(2,1)S(1)}, u32[]{:S(2)}, u32[]{:S(2)}) async-start(bf16[16,128,256]{2,1,0:T(8,128)(2,1)} %bitcast.9), calls=%async_computation.1 | async-start | bytes 2097152 | tf_op jit(solution)/shard_map/all_to_all | solution.py:390
  273.4 2.3 copy-start.8
Sparse Core Ops, SparseCore 0:
  39.8 156.2 all-gather.5
  197.9 36.8 all-gather.3
